TPU v7x, 512 devices: a whole 4x8x8 slice. The times are simulated.
512 devices in a mesh: row: 32 (over z, y_hi), col: 16 (over y_lo, x, core).
Axes of the slice: x: 4, y: 8 (y_hi: 4, y_lo: 2; y = y_hi * 2 + y_lo), z: 8, core: 2. Of those that a mesh axis runs over, the one named last changes fastest.
Arguments:
- panel_xyz: float32 [3, 65536], P(None, ('col', 'row')), may hold values from -1.2 to 1.2, as said below
- panel_weight: float32 [1, 65536], P(None, ('col', 'row')), may hold values from 0.3 to 3
- self_term: float32 [65536], P(('col', 'row')), may hold values from 2 to 6
- panel_slot: int32 [65536], P(('col', 'row')), may hold values from 0 to 127, as said below
- block_inverse: float32 [64, 65536], P(None, ('col', 'row')), may hold values from -0.75 to 0.75
- incident: float32 [16, 65536], P(None, ('col', 'row')), may hold values from -6 to 6
- field_xyz: float32 [3, 16384], P(None, 'row'), may hold values from -2.5 to 2.5
- field_group: int32 [16384], P(('row', 'col')), may hold values from 0 to 127
Outputs:
- density: float32 [16, 65536], P(None, ('col', 'row'))
- potential: bfloat16 [16, 16384], P(None, ('row', 'col'))
- detector: float32 [16, 128], replicated
Inputs may be any that keep to these rules, and one draw needn't show every extreme that they name: Within each aligned run of 128 panels, panel_slot is a permutation of 0 to 127. `panel_xyz`: panel centres lie on a closed surface around the anchor.
All inputs are finite; a program needn't handle non-finite values.
Results may differ from a plain program's by a relative error of at most 0.018.
Values may be sent and summed in bfloat16 or wider, within the bound.
A program may use at most 64 MiB of HBM per device.

v0:
```python
import math

import jax
import jax.numpy as jnp
from jax import lax
from jax.sharding import PartitionSpec as P

GROUPS = 128


wave_number = 12.0
smoothing = 0.05
damping = 0.5


def kernel_tile(targets, sources, source_weight, coupling):
    delta_x = targets[0][:, None] - sources[0][None, :]
    delta_y = targets[1][:, None] - sources[1][None, :]
    delta_z = targets[2][:, None] - sources[2][None, :]
    dist_sq = delta_x * delta_x + delta_y * delta_y + delta_z * delta_z
    radius = jnp.sqrt(dist_sq)
    entries = (
        coupling
        * source_weight[None, :]
        * jnp.cos(wave_number * radius)
        * lax.rsqrt(dist_sq + smoothing * smoothing)
    )
    return entries.astype(jnp.bfloat16)


def local_precondition(residual, panel_slot, block_inverse, self_term):
    block_size = block_inverse.shape[0]
    position = panel_slot % block_size
    block_of = panel_slot // block_size
    selector = (position[:, None] == jnp.arange(block_size, dtype=jnp.int32)[None, :]).astype(
        jnp.float32
    )
    chosen = jnp.dot(
        selector, block_inverse, precision=lax.Precision.HIGHEST, preferred_element_type=jnp.float32
    )
    coupled = jnp.where(block_of[:, None] == block_of[None, :], chosen, jnp.zeros_like(chosen))
    mixing = lax.dot_general(
        residual,
        coupled,
        (((1,), (1,)), ((), ())),
        precision=lax.Precision.HIGHEST,
        preferred_element_type=jnp.float32,
    )
    return residual / self_term[None, :] + mixing


def make_fold(targets, source_xyz, source_weight, coupling):

    def folding(running, portion, anchor):
        span_cols = portion.shape[1]
        block_cols = math.gcd(span_cols, 256)

        def advance(turn, partial_sum):
            offset = turn * block_cols
            density_block = lax.dynamic_slice_in_dim(portion, offset, block_cols, 1)
            source_block = lax.dynamic_slice_in_dim(source_xyz, offset, block_cols, 1)
            weight_block = lax.dynamic_slice_in_dim(source_weight, offset, block_cols, 1)
            kernel = kernel_tile(targets, source_block, weight_block[0], coupling)
            return partial_sum + lax.dot_general(
                density_block, kernel, (((1,), (1,)), ((), ())), preferred_element_type=jnp.float32
            )

        return lax.fori_loop(0, span_cols // block_cols, advance, running)

    return folding


def local(
    panel_xyz, panel_weight, self_term, panel_slot, block_inverse, incident, field_xyz, field_group
):
    row_count = lax.axis_size("row")
    col_count = lax.axis_size("col")
    shard_width = panel_xyz.shape[1]
    wave_count = incident.shape[0]
    coupling = 1.0 / math.sqrt(shard_width * row_count * col_count)
    down_xyz, down_weight = (
        lax.all_gather(panel_xyz, "row", axis=1, tiled=True),
        lax.all_gather(panel_weight, "row", axis=1, tiled=True),
    )
    across_xyz, across_weight = (
        lax.all_gather(panel_xyz, "col", axis=1, tiled=True),
        lax.all_gather(panel_weight, "col", axis=1, tiled=True),
    )
    start = local_precondition(incident, panel_slot, block_inverse, self_term)
    start_b = start.astype(jnp.bfloat16)
    folding = make_fold(down_xyz, across_xyz, across_weight, coupling)
    initial = jnp.zeros((wave_count, down_xyz.shape[1]), jnp.float32)
    partial_sum = folding(initial, lax.all_gather(start_b, "col", axis=1, tiled=True), jnp.int32(0))
    images = lax.psum_scatter(
        partial_sum.astype(jnp.bfloat16), "row", scatter_dimension=1, tiled=True
    ).astype(jnp.float32)
    residual = incident - self_term[None, :] * start - images
    density = start + damping * local_precondition(residual, panel_slot, block_inverse, self_term)
    density_b = density.astype(jnp.bfloat16)
    field_fold = make_fold(field_xyz, down_xyz, down_weight, coupling)
    field_initial = jnp.zeros((wave_count, field_xyz.shape[1]), jnp.float32)
    field_partial = field_fold(
        field_initial, lax.all_gather(density_b, "row", axis=1, tiled=True), jnp.int32(0)
    )
    field_sum = lax.psum_scatter(
        field_partial.astype(jnp.bfloat16), "col", scatter_dimension=1, tiled=True
    ).astype(jnp.float32)
    onehot = (field_group[:, None] == jnp.arange(GROUPS, dtype=jnp.int32)[None, :]).astype(
        jnp.float32
    )
    group_sums = jnp.dot(
        field_sum, onehot, precision=lax.Precision.HIGHEST, preferred_element_type=jnp.float32
    )
    fields = field_xyz.shape[1] * row_count
    detector = lax.psum(group_sums, ("row", "col")) / math.sqrt(fields / GROUPS)
    return (density, field_sum.astype(jnp.bfloat16), detector)


def solution(mesh):
    return jax.shard_map(
        local,
        mesh=mesh,
        in_specs=(
            P(None, ("col", "row")),
            P(None, ("col", "row")),
            P(("col", "row")),
            P(("col", "row")),
            P(None, ("col", "row")),
            P(None, ("col", "row")),
            P(None, "row"),
            P(("row", "col")),
        ),
        out_specs=(P(None, ("col", "row")), P(None, ("row", "col")), P()),
        check_vma=False,
    )
```

profile of v0, /device:TPU:1, one launch (start us, length us, event | category | flops | bytes accessed | tf_op | source)
XLA Modules:
  0.0 791.2 jit_solution(14344845842401207009)
XLA Ops:
  7.2 75.2 %all_gather.20 = f32[3,4096]{1,0:T(4,128)S(1)} all-gather(f32[3,128]{1,0:T(4,128)} %param.12), channel_id=1, replica_groups=mesh['row'=32,'col'=16] {'row'}, dimensions={1}, use_global_device_ids=true | all-gather | bytes 50688 | tf_op jit(solution)/shard_map/all_gather | solution.py:82
  82.5 33.7 %all_gather.21 = f32[3,2048]{1,0:T(4,128)S(1)} all-gather(f32[3,128]{1,0:T(4,128)} %param.12), channel_id=1, replica_groups=mesh['row'=32,'col'=16] {'col'}, dimensions={1}, use_global_device_ids=true | all-gather | bytes 26112 | tf_op jit(solution)/shard_map/all_gather | solution.py:86
  116.2 0.7 and_select_fusion.1
  116.9 0.2 convolution_select_fusion
  117.1 1.0 fusion.40
  118.1 16.4 %all_gather.18 = bf16[16,2048]{1,0:T(8,128)(2,1)S(1)} all-gather(bf16[16,128]{1,0:T(8,128)(2,1)S(1)} %get-tuple-element.305), channel_id=1, replica_groups=mesh['row'=32,'col'=16] {'col'}, dimensions={1}, use_global_device_ids=true | all-gather | bytes 69632 | tf_op jit(solution)/shard_map/all_gather | solution.py:93
  134.5 17.8 %all_gather.19 = f32[1,2048]{1,0:T(1,128)S(1)} all-gather(f32[1,128]{1,0:T(1,128)} %param.13), channel_id=1, replica_groups=mesh['row'=32,'col'=16] {'col'}, dimensions={1}, use_global_device_ids=true | all-gather | bytes 8704 | tf_op jit(solution)/shard_map/all_gather | solution.py:87
  152.3 133.3 %while.28 = (s32[]{:T(128)}, f32[16,4096]{1,0:T(8,128)S(1)}, bf16[16,2048]{1,0:T(8,128)(2,1)S(1)}, f32[1,2048]{1,0:T(1,128)S(1)}, f32[3,4096]{1,0:T(4,128)S(1)},...) while((s32[]{:T(128)}, f32[16,4096]{1,0:T(8,128)S(1)}, ...), condition=%wide.region_1.2_spmd.clone, body=%wide.region_0.1_spmd.clone.sunk | while | flops 47317256 | bytes 692445 | solution.py:68
  152.4 16.5 %convolution_add_fusion.5 = f32[16,4096]{1,0:T(8,128)S(1)} fusion(f32[256]{0:T(256)S(1)} %bitcast.67, f32[4096]{0:T(1024)S(1)} %bitcast.59, f32[256]{0:T(256)S(1)} %bitcast.66, f32[4096]{0:T(1024)S(1)} %bitcast.60, f32[256]{0:T(256)S(1)} %bitcast.65, f32[4096]{0:T(1024)S(1)} %bitcast.58, f32[256]{0:T(256)S(1)} %bitcast.68, ...), kind=kOutput, calls=%fused_computation.clone.1 | convolution fusion | flops 47316992 | bytes 585733 | tf_op jit(solution)/shard_map/while/body/eval_jaxpr/dot_general | solution.py:64
  168.9 0.1 constant_dynamic-slice_fusion.4
  169.0 16.5 %convolution_add_fusion.5 = f32[16,4096]{1,0:T(8,128)S(1)} fusion(f32[256]{0:T(256)S(1)} %bitcast.67, f32[4096]{0:T(1024)S(1)} %bitcast.59, f32[256]{0:T(256)S(1)} %bitcast.66, f32[4096]{0:T(1024)S(1)} %bitcast.60, f32[256]{0:T(256)S(1)} %bitcast.65, f32[4096]{0:T(1024)S(1)} %bitcast.58, f32[256]{0:T(256)S(1)} %bitcast.68, ...), kind=kOutput, calls=%fused_computation.clone.1 | convolution fusion | flops 47316992 | bytes 585733 | tf_op jit(solution)/shard_map/while/body/eval_jaxpr/dot_general | solution.py:64
  185.6 0.1 constant_dynamic-slice_fusion.4
  185.7 16.5 %convolution_add_fusion.5 = f32[16,4096]{1,0:T(8,128)S(1)} fusion(f32[256]{0:T(256)S(1)} %bitcast.67, f32[4096]{0:T(1024)S(1)} %bitcast.59, f32[256]{0:T(256)S(1)} %bitcast.66, f32[4096]{0:T(1024)S(1)} %bitcast.60, f32[256]{0:T(256)S(1)} %bitcast.65, f32[4096]{0:T(1024)S(1)} %bitcast.58, f32[256]{0:T(256)S(1)} %bitcast.68, ...), kind=kOutput, calls=%fused_computation.clone.1 | convolution fusion | flops 47316992 | bytes 585733 | tf_op jit(solution)/shard_map/while/body/eval_jaxpr/dot_general | solution.py:64
  202.2 0.1 constant_dynamic-slice_fusion.4
  202.3 16.5 %convolution_add_fusion.5 = f32[16,4096]{1,0:T(8,128)S(1)} fusion(f32[256]{0:T(256)S(1)} %bitcast.67, f32[4096]{0:T(1024)S(1)} %bitcast.59, f32[256]{0:T(256)S(1)} %bitcast.66, f32[4096]{0:T(1024)S(1)} %bitcast.60, f32[256]{0:T(256)S(1)} %bitcast.65, f32[4096]{0:T(1024)S(1)} %bitcast.58, f32[256]{0:T(256)S(1)} %bitcast.68, ...), kind=kOutput, calls=%fused_computation.clone.1 | convolution fusion | flops 47316992 | bytes 585733 | tf_op jit(solution)/shard_map/while/body/eval_jaxpr/dot_general | solution.py:64
  218.8 0.1 constant_dynamic-slice_fusion.4
  219.0 16.5 %convolution_add_fusion.5 = f32[16,4096]{1,0:T(8,128)S(1)} fusion(f32[256]{0:T(256)S(1)} %bitcast.67, f32[4096]{0:T(1024)S(1)} %bitcast.59, f32[256]{0:T(256)S(1)} %bitcast.66, f32[4096]{0:T(1024)S(1)} %bitcast.60, f32[256]{0:T(256)S(1)} %bitcast.65, f32[4096]{0:T(1024)S(1)} %bitcast.58, f32[256]{0:T(256)S(1)} %bitcast.68, ...), kind=kOutput, calls=%fused_computation.clone.1 | convolution fusion | flops 47316992 | bytes 585733 | tf_op jit(solution)/shard_map/while/body/eval_jaxpr/dot_general | solution.py:64
  235.5 0.1 constant_dynamic-slice_fusion.4
  235.6 16.5 %convolution_add_fusion.5 = f32[16,4096]{1,0:T(8,128)S(1)} fusion(f32[256]{0:T(256)S(1)} %bitcast.67, f32[4096]{0:T(1024)S(1)} %bitcast.59, f32[256]{0:T(256)S(1)} %bitcast.66, f32[4096]{0:T(1024)S(1)} %bitcast.60, f32[256]{0:T(256)S(1)} %bitcast.65, f32[4096]{0:T(1024)S(1)} %bitcast.58, f32[256]{0:T(256)S(1)} %bitcast.68, ...), kind=kOutput, calls=%fused_computation.clone.1 | convolution fusion | flops 47316992 | bytes 585733 | tf_op jit(solution)/shard_map/while/body/eval_jaxpr/dot_general | solution.py:64
  252.1 0.1 constant_dynamic-slice_fusion.4
  252.3 16.5 %convolution_add_fusion.5 = f32[16,4096]{1,0:T(8,128)S(1)} fusion(f32[256]{0:T(256)S(1)} %bitcast.67, f32[4096]{0:T(1024)S(1)} %bitcast.59, f32[256]{0:T(256)S(1)} %bitcast.66, f32[4096]{0:T(1024)S(1)} %bitcast.60, f32[256]{0:T(256)S(1)} %bitcast.65, f32[4096]{0:T(1024)S(1)} %bitcast.58, f32[256]{0:T(256)S(1)} %bitcast.68, ...), kind=kOutput, calls=%fused_computation.clone.1 | convolution fusion | flops 47316992 | bytes 585733 | tf_op jit(solution)/shard_map/while/body/eval_jaxpr/dot_general | solution.py:64
  268.8 0.1 constant_dynamic-slice_fusion.4
  268.9 16.5 %convolution_add_fusion.5 = f32[16,4096]{1,0:T(8,128)S(1)} fusion(f32[256]{0:T(256)S(1)} %bitcast.67, f32[4096]{0:T(1024)S(1)} %bitcast.59, f32[256]{0:T(256)S(1)} %bitcast.66, f32[4096]{0:T(1024)S(1)} %bitcast.60, f32[256]{0:T(256)S(1)} %bitcast.65, f32[4096]{0:T(1024)S(1)} %bitcast.58, f32[256]{0:T(256)S(1)} %bitcast.68, ...), kind=kOutput, calls=%fused_computation.clone.1 | convolution fusion | flops 47316992 | bytes 585733 | tf_op jit(solution)/shard_map/while/body/eval_jaxpr/dot_general | solution.py:64
  285.6 1.3 copy.11
  287.0 61.4 %all_gather.23 = f32[1,4096]{1,0:T(1,128)S(1)} all-gather(f32[1,128]{1,0:T(1,128)S(1)} %copy-done.4), channel_id=1, replica_groups=mesh['row'=32,'col'=16] {'row'}, dimensions={1}, use_global_device_ids=true | all-gather | bytes 16896 | tf_op jit(solution)/shard_map/all_gather | solution.py:83
  348.4 150.9 %reduce-scatter.7.cloned.1.call-done = bf16[128,16]{1,0:T(8,128)(2,1)} async-done(((bf16[4096,16]{1,0:T(8,128)(2,1)}), bf16[128,16]{1,0:T(8,128)(2,1)}) %reduce-scatter.7.cloned.1.call-update) | async-done | bytes 4112
  499.3 0.8 copy.12
  500.2 0.8 fusion.41
  501.0 65.6 %all_gather.22 = bf16[16,4096]{1,0:T(8,128)(2,1)S(1)} all-gather(bf16[16,128]{1,0:T(8,128)(2,1)S(1)} %get-tuple-element.307), channel_id=1, replica_groups=mesh['row'=32,'col'=16] {'row'}, dimensions={1}, use_global_device_ids=true | all-gather | bytes 135168 | tf_op jit(solution)/shard_map/all_gather | solution.py:103
  566.6 37.8 %while.29 = (s32[]{:T(128)}, f32[16,512]{1,0:T(8,128)S(1)}, bf16[16,4096]{1,0:T(8,128)(2,1)S(1)}, f32[1,4096]{1,0:T(1,128)S(1)}, f32[3,512]{1,0:T(4,128)S(1)}, /...) while((s32[]{:T(128)}, f32[16,512]{1,0:T(8,128)S(1)}, ...), condition=%wide.region_4.5_spmd.clone, body=%wide.region_3.4_spmd.clone.sunk | while | flops 5914889 | bytes 104669 | solution.py:68
  566.7 2.3 convolution_add_fusion.6
  569.0 0.1 constant_dynamic-slice_fusion.5
  569.0 2.3 convolution_add_fusion.6
  571.3 0.1 constant_dynamic-slice_fusion.5
  571.4 2.3 convolution_add_fusion.6
  573.7 0.1 constant_dynamic-slice_fusion.5
  573.8 2.3 convolution_add_fusion.6
  576.0 0.1 constant_dynamic-slice_fusion.5
  576.1 2.3 convolution_add_fusion.6
  578.4 0.1 constant_dynamic-slice_fusion.5
  578.5 2.3 convolution_add_fusion.6
  580.8 0.1 constant_dynamic-slice_fusion.5
  580.9 2.3 convolution_add_fusion.6
  583.1 0.1 constant_dynamic-slice_fusion.5
  583.2 2.3 convolution_add_fusion.6
  585.5 0.1 constant_dynamic-slice_fusion.5
  585.6 2.3 convolution_add_fusion.6
  587.9 0.1 constant_dynamic-slice_fusion.5
  588.0 2.3 convolution_add_fusion.6
  590.2 0.1 constant_dynamic-slice_fusion.5
  590.3 2.3 convolution_add_fusion.6
  592.6 0.1 constant_dynamic-slice_fusion.5
  592.7 2.3 convolution_add_fusion.6
  595.0 0.1 constant_dynamic-slice_fusion.5
  595.0 2.3 convolution_add_fusion.6
  597.4 2.3 convolution_add_fusion.6
  599.8 2.3 convolution_add_fusion.6
  602.1 2.3 convolution_add_fusion.6
  604.4 0.8 copy.13
  605.2 76.0 %reduce-scatter.9.cloned.1.call-done = bf16[32,16]{1,0:T(8,128)(2,1)} async-done(((bf16[512,16]{1,0:T(8,128)(2,1)}), bf16[32,16]{1,0:T(8,128)(2,1)}) %reduce-scatter.9.cloned.1.call-update) | async-done | bytes 1040
  681.2 1.4 copy.14
  682.6 0.9 fusion.30
  683.4 100.3 %psum.7 = f32[16,128]{1,0:T(8,128)S(1)} all-reduce(f32[16,128]{1,0:T(8,128)S(1)} %fusion.30), channel_id=1, replica_groups=mesh['row'=32,'col'=16] {'row','col'}, use_global_device_ids=true, to_apply=%region_6.7 | all-reduce | flops 2048 | bytes 16384 | tf_op jit(solution)/shard_map/psum | solution.py:115
  783.8 0.6 broadcast_multiply_fusion
  (49 shorter events, 0.9 us)
Async XLA Ops:
  7.2 109.7 %copy-start = (f32[64,128]{1,0:T(8,128)S(1)}, f32[64,128]{1,0:T(8,128)}, u32[]{:S(2)}) copy-start(f32[64,128]{1,0:T(8,128)} %param.16) | copy-start | bytes 98308
  7.2 492.2 %reduce-scatter.7.cloned.1.call-start = ((), (), s32[]{:S(2)}) async-start(), calls=%async_computation.2 | async-start | bytes 1081344
  285.6 1.5 copy-start.4
  285.6 214.6 %copy-start.2 = (f32[16,128]{1,0:T(8,128)S(1)}, f32[16,128]{1,0:T(8,128)}, u32[]{:S(2)}) copy-start(f32[16,128]{1,0:T(8,128)} %param.17) | copy-start | bytes 24580
  285.6 214.6 %copy-start.3 = (f32[128]{0:T(128)S(1)}, f32[128]{0:T(128)}, u32[]{:S(2)}) copy-start(f32[128]{0:T(128)} %param.14) | copy-start | bytes 1540
  285.6 281.0 %copy-start.1 = (f32[3,512]{1,0:T(4,128)S(1)}, f32[3,512]{1,0:T(4,128)}, u32[]{:S(2)}) copy-start(f32[3,512]{1,0:T(4,128)} %param.18) | copy-start | bytes 18436
  287.0 394.2 %reduce-scatter.9.cloned.1.call-start = ((), (), s32[]{:S(2)}) async-start(), calls=%async_computation.3 | async-start | bytes 139264
  566.6 116.0 %copy-start.5 = (s32[32]{0:T(128)S(1)}, s32[32]{0:T(128)}, u32[]{:S(2)}) copy-start(s32[32]{0:T(128)} %param.19) | copy-start | bytes 388
Sparse Core Ops, SparseCore 0:
  287.1 212.2 reduce-scatter.6
  605.3 75.8 reduce-scatter.8
where the time goes:
time: 792 us; the launch traced here: 791 us
  blocking collectives  370 us (47%)
  waiting for transfers between devices  227 us (29%)
  matrix products  171 us (22%)
  between operations  14.1 us (2%)
    unnamed x4, waiting for transfers between devices  227 us
    dot_general x24, matrix products, advance(): lax.dot_general(density_block, kernel, (((1,), (1,)), ((), ())), preferre...  169 us
    psum x1, blocking collectives, local(): detector = lax.psum(group_sums, ('row', 'col')) / math.sqrt(fields / GROUPS)  100 us
    all_gather x1, blocking collectives, local(): lax.all_gather(panel_xyz, 'row', axis=1, tiled=True)  75.2 us
    all_gather x1, blocking collectives, local(): lax.all_gather(density_b, 'row', axis=1, tiled=True)  65.6 us
    all_gather x1, blocking collectives, local(): lax.all_gather(panel_weight, 'row', axis=1, tiled=True)  61.4 us
    all_gather x1, blocking collectives, local(): lax.all_gather(panel_xyz, 'col', axis=1, tiled=True)  33.7 us
    all_gather x1, blocking collectives, local(): lax.all_gather(panel_weight, 'col', axis=1, tiled=True)  17.8 us
  transfers between devices with their start and end apart: 2, of which 2 were waited for; matrix products, arithmetic and copies ran while one was open for 0% of the time, Pallas kernels for 0%

commit v1 on v0

v1 whole, which is shorter than its diff:
```python
import functools
import math

import jax
import jax.numpy as jnp
import numpy as np
from jax import lax
from jax.experimental import pallas as pl
from jax.experimental.pallas import tpu as pltpu
from jax.sharding import PartitionSpec as P

MESH = pl.DeviceIdType.MESH
HIGHEST = lax.Precision.HIGHEST
F32 = jnp.float32
BF16 = jnp.bfloat16

GROUPS = 128
SH = 128
WV = 16
FD = 32
wave_number = 12.0
smoothing = 0.05
damping = 0.5

B0, B1, B2, B3 = 6.283164041181243, -41.33714186520903, 81.3407492682057, -70.99322232997507
CYCLES = wave_number / (2.0 * math.pi)
EPS = smoothing * smoothing * CYCLES * CYCLES


def selectors():
    sel_b = np.zeros((16, 32), np.float32)
    sel_a = np.zeros((32, 16), np.float32)
    high, mid, low = 0, 1, 2
    pairs = [(high, high), (high, mid), (mid, high), (mid, mid), (high, low), (low, high), (mid, low), (low, mid)]
    k = 0
    for b, a in pairs:
        for c in range(3):
            sel_b[3 * b + c, k] = -2.0
            sel_a[k, 3 * a + c] = 1.0
            k += 1
    for n in range(3):
        sel_b[9 + n, k] = 1.0
        sel_a[k, 12] = 1.0
        k += 1
    for n in range(3):
        sel_b[12, k] = 1.0
        sel_a[k, 9 + n] = 1.0
        k += 1
    return sel_b, sel_a


def split3(x):
    h = x.astype(BF16).astype(F32)
    m = (x - h).astype(BF16).astype(F32)
    return h, m, (x - h) - m


def geometry(scr, xyz):
    c = xyz * CYCLES
    h, m, l = split3(c)
    nh, nm, nl = split3(jnp.sum(c * c, axis=0, keepdims=True))
    scr[0:3, :] = h
    scr[3:6, :] = m
    scr[6:9, :] = l
    scr[9:10, :] = nh
    scr[10:11, :] = nm
    scr[11:12, :] = nl
    scr[12:13, :] = jnp.ones_like(nh)
    scr[13:16, :] = jnp.zeros((3, c.shape[1]), F32)
    return scr[...].astype(BF16)


def pair_values(d):
    s = jnp.maximum(d, 1e-12)
    r = s * lax.rsqrt(s)
    v = 0.25 - jnp.abs(r - jnp.round(r))
    q = v * v
    p = ((q + B2 / B3) * q + B1 / B3) * q + B0 / B3
    return ((p * v) * lax.rsqrt(s + EPS)).astype(BF16)


def kernel(
    nz, ny, nc, scale, wave_scale,
    xyz, weight, self_term, slot, binv, inc, fxyz, fgroup, sel_b, sel_a,
    den_o, pot_o, det_o,
    geo_s, fgeo_s, fg_s, src, tgt, feat_a, feat_f, coupled, acc, rs_out, rs_in, den, gf, facc,
    pot_out, pot_in, fgs, det1, det2,
    src_ss, src_rs, tgt_ss, tgt_rs, rs_ss, rs_rs, den_ss, den_rs, pot_ss, pot_rs, fg_ss, fg_rs,
    d1_ss, d1_rs, d2_ss, d2_rs,
):
    nr = nz * ny
    fb = facc.shape[1] // 128
    i = lax.axis_index("row")
    j = lax.axis_index("col")
    iz, iy = i // ny, i % ny

    def hops(d):
        dz, dy = d
        return min(dz, nz - dz) + 2 * min(dy, ny - dy)

    offsets = sorted(((dz, dy) for dz in range(nz) for dy in range(ny)), key=hops)

    barrier = pltpu.get_barrier_semaphore()

    def greet_row(n, _):
        pl.semaphore_signal(barrier, inc=1, device_id=(lax.rem(i + n, nr), j), device_id_type=MESH)
        return 0

    def greet_col(n, _):
        pl.semaphore_signal(barrier, inc=1, device_id=(i, lax.rem(j + n, nc)), device_id_type=MESH)
        return 0

    lax.fori_loop(1, nr, greet_row, 0)
    lax.fori_loop(1, nc, greet_col, 0)

    packet = geometry(geo_s, xyz[...])
    src[0, 0:16, :] = packet
    tgt[0] = packet
    place = lax.broadcasted_iota(jnp.int32, (64, SH), 0)
    chosen = (place == slot[...] % 64).astype(F32)
    half = (lax.broadcasted_iota(jnp.int32, (8, SH), 0) == slot[...] // 64).astype(F32)
    over_rows = (((0,), (0,)), ((), ()))
    picked = lax.dot_general(binv[...], chosen, over_rows, precision=HIGHEST, preferred_element_type=F32)
    same = lax.dot_general(half, half, over_rows, preferred_element_type=F32)
    coupled[...] = picked * same

    def precondition(values):
        mixing = jnp.dot(values, coupled[...], precision=HIGHEST, preferred_element_type=F32)
        return values / self_term[...] + mixing

    start = precondition(inc[...])
    src[0, 16:32, :] = (start * weight[...]).astype(BF16)
    fg_s[...] = jnp.zeros_like(fg_s)
    fg_s[:, 0:FD] = jnp.broadcast_to(fgroup[...].astype(F32), (8, FD))
    fgs[j] = fg_s[...]

    pl.semaphore_wait(barrier, nr + nc - 2)

    def row_copy(k, src_ref, dst_ref, ss, rs):
        dz, dy = offsets[k]
        peer = lax.rem(iz + (nz - dz), nz) * ny + lax.rem(iy + (ny - dy), ny)
        return pltpu.make_async_remote_copy(
            src_ref=src_ref, dst_ref=dst_ref, send_sem=ss.at[k], recv_sem=rs.at[k],
            device_id=(peer, j), device_id_type=MESH,
        )

    def col_copy(k, src_ref, dst_ref, ss, rs, sem):
        return pltpu.make_async_remote_copy(
            src_ref=src_ref, dst_ref=dst_ref, send_sem=ss.at[k], recv_sem=rs.at[sem],
            device_id=(i, lax.rem(j + k, nc)), device_id_type=MESH,
        )

    def each(lo, hi, body):
        def step(n, _):
            body(n)
            return 0

        lax.fori_loop(lo, hi, step, 0)

    each(1, nc, lambda k: col_copy(k, tgt.at[0], tgt.at[k], tgt_ss, tgt_rs, k).start())
    for k in range(nr - 1, 0, -1):
        row_copy(k, src.at[0], src.at[k], src_ss, src_rs).start()
    each(1, nc, lambda k: col_copy(k, fgs.at[j], fgs.at[j], fg_ss, fg_rs, k).start())

    def features_a(pk):
        return jnp.dot(sel_a[...], pk, preferred_element_type=F32).astype(BF16)

    def features_b(pk):
        return lax.dot_general(pk, sel_b[...], over_rows, preferred_element_type=F32).astype(BF16)

    feat_f[...] = features_a(geometry(fgeo_s, fxyz[...]))
    acc[...] = jnp.zeros_like(acc)

    def tgt_wait(k):
        col_copy(0, tgt.at[0], tgt.at[k], tgt_ss, tgt_rs, k).wait_recv()
        feat_a[:, pl.ds(pl.multiple_of(k * SH, SH), SH)] = features_a(tgt[k])

    feat_a[:, 0:SH] = features_a(tgt[0])
    each(1, nc, tgt_wait)

    def plain_wait(k, buf, rs):
        pltpu.make_async_remote_copy(
            src_ref=buf.at[0], dst_ref=buf.at[0], send_sem=rs.at[k], recv_sem=rs.at[k],
            device_id=(i, j), device_id_type=MESH,
        ).wait_recv()

    tb = min(1024, nc * SH)

    def images_chunk(c):
        @pl.when(c > 0)
        def _():
            plain_wait(2 * c, src, src_rs)

        plain_wait(2 * c + 1, src, src_rs)
        one, two = src[2 * c], src[2 * c + 1]
        b = features_b(jnp.concatenate([one[0:16], two[0:16]], axis=1))
        x = jnp.concatenate([one[16:32], two[16:32]], axis=1)

        def tile(t):
            cols = pl.ds(pl.multiple_of(t * tb, tb), tb)
            g = pair_values(jnp.dot(b, feat_a[:, cols], preferred_element_type=F32))
            acc[:, cols] += jnp.dot(x, g, preferred_element_type=F32)

        each(0, nc * SH // tb, tile)

    each(0, nr // 2, images_chunk)

    def rs_send(k):
        rs_out[k] = acc[:, pl.ds(pl.multiple_of(k * SH, SH), SH)].astype(BF16)
        back = lax.rem(nc - k, nc)
        pltpu.make_async_remote_copy(
            src_ref=rs_out.at[k], dst_ref=rs_in.at[k], send_sem=rs_ss.at[k], recv_sem=rs_rs.at[k],
            device_id=(i, lax.rem(j + back, nc)), device_id_type=MESH,
        ).start()

    each(1, nc, rs_send)

    def field_chunk(c):
        one, two = src[2 * c], src[2 * c + 1]
        b = features_b(jnp.concatenate([one[0:16], two[0:16]], axis=1))
        gf[c] = pair_values(jnp.dot(b, feat_f[...], preferred_element_type=F32))

    early = nr // 2 * 3 // 8
    each(0, early, field_chunk)

    rs_in[0] = jnp.zeros((WV, SH), BF16)
    each(1, nc, lambda k: plain_wait(k, rs_in, rs_rs))
    total = acc[:, 0:SH] + jnp.sum(rs_in[...].astype(F32), axis=0)
    residual = inc[...] - self_term[...] * start - total * scale
    density = start + damping * precondition(residual)
    den_o[...] = density
    den[0] = (density * weight[...]).astype(BF16)
    for k in range(nr - 1, 0, -1):
        row_copy(k, den.at[0], den.at[k], den_ss, den_rs).start()

    each(early, nr // 2, field_chunk)
    facc[...] = jnp.zeros_like(facc)

    def field_sum(c):
        @pl.when(c > 0)
        def _():
            plain_wait(2 * c, den, den_rs)

        plain_wait(2 * c + 1, den, den_rs)
        x = jnp.concatenate([den[2 * c], den[2 * c + 1]], axis=1)
        facc[...] += jnp.dot(x, gf[c], preferred_element_type=F32)

    each(0, nr // 2, field_sum)

    facc[...] = facc[...] * scale
    for b in range(fb):
        pot_out[b] = facc[:, b * 128:(b + 1) * 128].astype(BF16)

    each(1, nc, lambda k: col_copy(k, fgs.at[j], fgs.at[j], fg_ss, fg_rs, k).wait_recv())
    each(1, nc, lambda k: col_copy(k, pot_out.at[lax.rem(j + k, nc) // 4], pot_in.at[k], pot_ss, pot_rs, k).start())

    part = jnp.zeros((WV, GROUPS), F32)
    detectors = lax.broadcasted_iota(jnp.int32, (GROUPS, 128), 0).astype(F32)
    for b in range(fb):
        groups = fgs[4 * b]
        for m in range(1, 4):
            groups = groups + pltpu.roll(fgs[4 * b + m], FD * m, 1)
        onehot = (detectors == groups[0:1, :]).astype(F32)
        part = part + lax.dot_general(
            facc[:, b * 128:(b + 1) * 128], onehot, (((1,), (1,)), ((), ())), precision=HIGHEST, preferred_element_type=F32
        )
    det1[j] = part
    each(1, nc, lambda k: col_copy(k, det1.at[j], det1.at[j], d1_ss, d1_rs, k).start())

    pot_in[0] = pot_out[j // 4]
    each(1, nc, lambda k: plain_wait(k, pot_in, pot_rs))
    pot = jnp.sum(pot_in[...].astype(F32), axis=0)
    pot = pltpu.roll(pot, lax.rem(128 - FD * lax.rem(j, 4), 128), 1)
    pot_o[...] = pot[:, 0:FD].astype(BF16)

    each(1, nc, lambda k: plain_wait(k, det1, d1_rs))
    det2[i] = jnp.sum(det1[...], axis=0)
    for k in range(nr - 1, 0, -1):
        row_copy(k, det2.at[i], det2.at[i], d2_ss, d2_rs).start()
    each(1, nr, lambda k: plain_wait(k, det2, d2_rs))
    det_o[...] = jnp.sum(det2[...], axis=0) * wave_scale

    def sent(n, buf, ss):
        def wait(k):
            pltpu.make_async_remote_copy(
                src_ref=buf.at[0], dst_ref=buf.at[0], send_sem=ss.at[k], recv_sem=ss.at[k],
                device_id=(i, j), device_id_type=MESH,
            ).wait_send()

        each(1, n, wait)

    sent(nc, tgt, tgt_ss)
    sent(nr, src, src_ss)
    sent(nc, fgs, fg_ss)
    sent(nc, rs_out, rs_ss)
    sent(nr, den, den_ss)
    sent(nc, pot_out, pot_ss)
    sent(nc, det1, d1_ss)
    sent(nr, det2, d2_ss)


def local(
    nz, ny, nc, panel_xyz, panel_weight, self_term, panel_slot, block_inverse, incident, field_xyz, field_group
):
    nr = nz * ny
    panels = SH * nr * nc
    fields = field_xyz.shape[1]
    scale = CYCLES * B3 / math.sqrt(panels)
    wave_scale = 1.0 / math.sqrt(fields * nr / GROUPS)
    sel_b, sel_a = selectors()
    vmem, dma = pltpu.VMEM, pltpu.SemaphoreType.DMA
    whole = pl.BlockSpec(memory_space=pltpu.VMEM)
    sems = []
    for n in (nr, nc, nc, nr, nc, nc, nc, nr):
        sems += [dma((n,)), dma((n,))]
    return pl.pallas_call(
        functools.partial(kernel, nz, ny, nc, scale, wave_scale),
        out_shape=(
            jax.ShapeDtypeStruct((WV, SH), F32),
            jax.ShapeDtypeStruct((WV, FD), BF16),
            jax.ShapeDtypeStruct((WV, GROUPS), F32),
        ),
        in_specs=[whole] * 10,
        out_specs=(whole,) * 3,
        scratch_shapes=[
            vmem((16, SH), F32),
            vmem((16, fields), F32),
            vmem((8, 128), F32),
            vmem((nr, 32, SH), BF16),
            vmem((nc, 16, SH), BF16),
            vmem((32, nc * SH), BF16),
            vmem((32, fields), BF16),
            vmem((SH, SH), F32),
            vmem((WV, nc * SH), F32),
            vmem((nc, WV, SH), BF16),
            vmem((nc, WV, SH), BF16),
            vmem((nr, WV, SH), BF16),
            vmem((nr // 2, 2 * SH, fields), BF16),
            vmem((WV, fields), F32),
            vmem((fields // 128, WV, 128), BF16),
            vmem((nc, WV, 128), BF16),
            vmem((nc, 8, 128), F32),
            vmem((nc, WV, GROUPS), F32),
            vmem((nr, WV, GROUPS), F32),
        ] + sems,
        compiler_params=pltpu.CompilerParams(
            collective_id=0, has_side_effects=True, vmem_limit_bytes=48 * 1024 * 1024
        ),
    )(
        panel_xyz, panel_weight, self_term.reshape(1, SH), panel_slot.reshape(1, SH), block_inverse, incident,
        field_xyz, field_group.reshape(1, FD), jnp.asarray(sel_b, BF16), jnp.asarray(sel_a, BF16),
    )


def solution(mesh):
    nr, nc = mesh.shape["row"], mesh.shape["col"]
    ny = 4 if nr % 8 == 0 else 2
    return jax.shard_map(
        functools.partial(local, nr // ny, ny, nc),
        mesh=mesh,
        in_specs=(
            P(None, ("col", "row")),
            P(None, ("col", "row")),
            P(("col", "row")),
            P(("col", "row")),
            P(None, ("col", "row")),
            P(None, ("col", "row")),
            P(None, "row"),
            P(("row", "col")),
        ),
        out_specs=(P(None, ("col", "row")), P(None, ("row", "col")), P()),
        check_vma=False,
    )
```

time: 792 us -> 93.7 us (0.12)
  blocking collectives: 370 us -> 0 us
  waiting for transfers between devices: 227 us -> 0 us
  matrix products: 171 us -> 0 us
  Pallas kernels: 0 us -> 86 us
  between operations: 14.1 us -> 0.68 us
    all_gather x6 -> x0, blocking collectives: 270 us -> none  [the longest x1 75.2 us: local(): lax.all_gather(panel_xyz, 'row', axis=1, tiled=True)]
    unnamed x4 -> x0, waiting for transfers between devices: 227 us -> none
    dot_general x28 -> x0, matrix products: 171 us -> none  [the longest x24 169 us: advance(): lax.dot_general(density_block, kernel, (((1,), (1,)), ((), ())), preferre...]
    psum x1 -> x0, blocking collectives: 100 us -> none  [local(): detector = lax.psum(group_sums, ('row', 'col')) / math.sqrt(fields / GROUPS)]
    pallas_call x0 -> x1, Pallas kernels: none -> 86 us  [local(): pl.pallas_call(functools.partial(kernel, nz, ny, nc, scale, wave_scale),...]
  transfers between devices with their start and end apart: 2 -> 0, of which waited for: 2 -> 0; matrix products, arithmetic and copies ran while one was open for 0% -> 0% of each run, Pallas kernels for 0% -> 0%
where the time goes in v1:
time: 93.7 us; the launch traced here: 93.3 us
  Pallas kernels  86 us (92%)
  local copies, waits for them, and re-layouts  6.65 us (7%)
    pallas_call x1, Pallas kernels, local(): pl.pallas_call(functools.partial(kernel, nz, ny, nc, scale, wave_scale),...  86 us
    unnamed x23, local copies, waits for them, and re-layouts  6.65 us

profile of v1, /device:TPU:1, one launch (start us, length us, event | category | flops | bytes accessed | tf_op | source)
XLA Modules:
  0.0 93.3 jit_solution(12854760450060392861)
XLA Ops:
  0.6 0.0 copy-start.4
  0.6 0.0 copy-start.6
  0.7 0.0 copy-start.7
  0.7 0.0 copy-start.8
  0.7 0.6 copy-done.4
  1.3 0.0 copy-done.6
  1.3 0.0 copy-done.7
  1.3 0.0 copy-done.8
  1.3 0.0 copy-start
  1.3 0.8 copy-done
  2.1 0.0 copy-start.1
  2.1 0.7 copy-done.1
  2.8 0.0 copy-start.2
  2.8 0.7 copy-done.2
  3.5 0.0 copy-start.3
  3.5 0.7 copy-done.3
  4.2 0.0 copy-start.5
  4.2 0.7 copy-done.5
  4.9 0.0 copy-start.9
  4.9 0.7 copy-done.9
  5.5 86.0 %shard_map.121 = (f32[16,128]{1,0:T(8,128)S(1)}, bf16[16,32]{1,0:T(8,128)(2,1)S(1)}, f32[16,128]{1,0:T(8,128)S(1)}) custom-call(f32[3,128]{1,0:T(4,128)S(1)} %copy-done.5, f32[1,128]{1,0:T(1,128)S(1)} %copy-done.6, f32[1,128]{1,0:T(1,128)S(1)} %bitcast.3, s32[1,128]{1,0:T(1,128)S(1)} %bitcast.4, f32[64,128]{1,0:T(8,128)S(1)} %copy-done, ...), custom_call_target="tpu_custom_call" | custom-call | tf_op jit(solution)/shard_map/pallas_call | solution.py:316
  91.5 0.6 copy.16
  92.1 0.6 copy.17
  92.7 0.6 copy.18
Async XLA Ops:
  0.6 0.7 copy-start.4
  0.6 0.7 copy-start.6
  0.7 0.7 copy-start.7
  0.7 0.7 copy-start.8
  1.3 0.8 copy-start
  2.1 0.7 copy-start.1
  2.8 0.7 copy-start.2
  3.5 0.7 copy-start.3
  4.2 0.7 copy-start.5
  4.9 0.7 copy-start.9

commit v2 on v1

v2 whole, which is shorter than its diff:
```python
import functools
import math

import jax
import jax.numpy as jnp
import numpy as np
from jax import lax
from jax.experimental import pallas as pl
from jax.experimental.pallas import tpu as pltpu
from jax.sharding import PartitionSpec as P

MESH = pl.DeviceIdType.MESH
HIGHEST = lax.Precision.HIGHEST
F32 = jnp.float32
BF16 = jnp.bfloat16

GROUPS = 128
SH = 128
WV = 16
FD = 32
wave_number = 12.0
smoothing = 0.05
damping = 0.5

B0, B1, B2, B3 = 6.283164041181243, -41.33714186520903, 81.3407492682057, -70.99322232997507
CYCLES = wave_number / (2.0 * math.pi)
EPS = smoothing * smoothing * CYCLES * CYCLES


def selectors():
    sel_b = np.zeros((16, 32), np.float32)
    sel_a = np.zeros((32, 16), np.float32)
    high, mid, low = 0, 1, 2
    pairs = [(high, high), (high, mid), (mid, high), (mid, mid), (high, low), (low, high), (mid, low), (low, mid)]
    k = 0
    for b, a in pairs:
        for c in range(3):
            sel_b[3 * b + c, k] = -2.0
            sel_a[k, 3 * a + c] = 1.0
            k += 1
    for n in range(3):
        sel_b[9 + n, k] = 1.0
        sel_a[k, 12] = 1.0
        k += 1
    for n in range(3):
        sel_b[12, k] = 1.0
        sel_a[k, 9 + n] = 1.0
        k += 1
    return sel_b, sel_a


def split3(x):
    h = x.astype(BF16).astype(F32)
    m = (x - h).astype(BF16).astype(F32)
    return h, m, (x - h) - m


def pieces(coords):
    parts = [split3(c) for c in coords]
    norm = split3(coords[0] * coords[0] + coords[1] * coords[1] + coords[2] * coords[2])
    rows = [parts[c][p] for p in range(3) for c in range(3)]
    return rows + list(norm) + [jnp.ones_like(norm[0])]


def pair_values(d):
    s = jnp.maximum(d, 1e-12)
    r = s * lax.rsqrt(s)
    v = 0.25 - jnp.abs(r - jnp.round(r))
    q = v * v
    p = ((q + B2 / B3) * q + B1 / B3) * q + B0 / B3
    return ((p * v) * lax.rsqrt(s + EPS)).astype(BF16)


def kernel(
    nz, ny, nc, scale, wave_scale,
    xyz_h, weight_h, self_h, slot_h, binv_h, inc_h, fxyz_h, fgroup_h, sel_b_h, sel_a_h,
    den_o, pot_o, det_o,
    xyz, weight, self_term, slot, binv, inc, fxyz, fgroup, sel_b, sel_a,
    geo_s, fs, src, tgt, feat_a, xt, coupled, acc, rsr_out, rsr_in, rs_out, rs_in, fpk, fgeo, onehot,
    den, gf, facc, pot_out, pot_in, det1, det2,
    load_s, src_ss, src_rs, tgt_ss, tgt_rs, rsr_ss, rsr_rs, rs_ss, rs_rs, den_ss, den_rs, fpk_ss, fpk_rs,
    pot_ss, pot_rs, d1_ss, d1_rs, d2_ss, d2_rs,
):
    nr = nz * ny
    i = lax.axis_index("row")
    j = lax.axis_index("col")
    iz, iy = i // ny, i % ny
    order, two_way, own = plan(nz, ny)
    chunks = len(order) // 2

    def each(lo, hi, body):
        def step(n, _):
            body(n)
            return 0

        lax.fori_loop(lo, hi, step, 0)

    barrier = pltpu.get_barrier_semaphore()
    each(1, nr, lambda n: pl.semaphore_signal(
        barrier, inc=1, device_id=(lax.rem(i + n, nr), j), device_id_type=MESH))
    each(1, nc, lambda n: pl.semaphore_signal(
        barrier, inc=1, device_id=(i, lax.rem(j + n, nc)), device_id_type=MESH))

    loads = [
        pltpu.make_async_copy(a, b, load_s.at[n])
        for n, (a, b) in enumerate([
            (xyz_h, xyz), (weight_h, weight), (self_h, self_term), (slot_h, slot), (binv_h, binv), (inc_h, inc),
            (fxyz_h, fxyz), (fgroup_h, fgroup), (sel_b_h, sel_b), (sel_a_h, sel_a),
        ])
    ]
    for load in loads:
        load.start()
    for load in loads:
        load.wait()

    rows = pieces([xyz[c:c + 1, :] * CYCLES for c in range(3)])
    for n, row in enumerate(rows):
        geo_s[n:n + 1, :] = row
    geo_s[13:16, :] = jnp.zeros((3, SH), F32)
    packet = geo_s[...].astype(BF16)
    src[own, 0:16, :] = packet
    tgt[0, 0:16, :] = packet
    place = lax.broadcasted_iota(jnp.int32, (64, SH), 0)
    chosen = (place == slot[...] % 64).astype(F32)
    half = (lax.broadcasted_iota(jnp.int32, (8, SH), 0) == slot[...] // 64).astype(F32)
    over_rows = (((0,), (0,)), ((), ()))
    over_lanes = (((1,), (1,)), ((), ()))
    picked = lax.dot_general(binv[...], chosen, over_rows, precision=HIGHEST, preferred_element_type=F32)
    same = lax.dot_general(half, half, over_rows, preferred_element_type=F32)
    coupled[...] = picked * same

    def precondition(values):
        mixing = jnp.dot(values, coupled[...], precision=HIGHEST, preferred_element_type=F32)
        return values / self_term[...] + mixing

    start = precondition(inc[...])
    start_w = (start * weight[...]).astype(BF16)
    src[own, 16:32, :] = start_w
    tgt[0, 16:32, :] = start_w

    lane = lax.broadcasted_iota(jnp.int32, (8, 128), 1)
    fs[...] = jnp.zeros_like(fs)
    fs[0, 0:3, :] = fxyz[:, pl.ds(pl.multiple_of(j // 4 * 128, 128), 128)]
    fs[1, 0:1, 0:FD] = fgroup[...].astype(F32)
    points = pltpu.roll(fs[0], lax.rem(128 - FD * lax.rem(j, 4), 128), 1)
    points = jnp.where(lane < FD, points, 0.0)
    row = points[0:1] + pltpu.roll(points, FD, 1)[1:2] + pltpu.roll(points, 2 * FD, 1)[2:3]
    row = row + pltpu.roll(fs[1], 3 * FD, 1)[0:1]
    mine = iy * nz + iz
    fpk[mine] = row

    pl.semaphore_wait(barrier, nr + nc - 2)

    def row_copy(d, k, src_ref, dst_ref, ss, rs):
        dz, dy = d
        peer = lax.rem(iz + dz % nz, nz) * ny + lax.rem(iy + dy % ny, ny)
        return pltpu.make_async_remote_copy(
            src_ref=src_ref, dst_ref=dst_ref, send_sem=ss.at[k], recv_sem=rs.at[k],
            device_id=(peer, j), device_id_type=MESH,
        )

    def col_copy(k, src_ref, dst_ref, ss, rs):
        return pltpu.make_async_remote_copy(
            src_ref=src_ref, dst_ref=dst_ref, send_sem=ss.at[k], recv_sem=rs.at[k],
            device_id=(i, lax.rem(j + k, nc)), device_id_type=MESH,
        )

    def arrived(k, buf, rs):
        pltpu.make_async_remote_copy(
            src_ref=buf.at[0], dst_ref=buf.at[0], send_sem=rs.at[k], recv_sem=rs.at[k],
            device_id=(i, j), device_id_type=MESH,
        ).wait_recv()

    each(1, nc, lambda k: col_copy(k, tgt.at[0], tgt.at[k], tgt_ss, tgt_rs).start())
    for k, (dz, dy) in enumerate(order):
        if k != own:
            row_copy((-dz, -dy), k, src.at[own], src.at[k], src_ss, src_rs).start()
    others = [(dz, dy) for dz in range(nz) for dy in range(ny)][1:]
    for k, d in enumerate(others):
        row_copy(d, k, fpk.at[mine], fpk.at[mine], fpk_ss, fpk_rs).start()

    def features_a(pk):
        return jnp.dot(sel_a[...], pk, preferred_element_type=F32).astype(BF16)

    def features_b(pk):
        return lax.dot_general(pk, sel_b[...], over_rows, preferred_element_type=F32).astype(BF16)

    acc[...] = jnp.zeros_like(acc)

    def take_target(k):
        cols = pl.ds(pl.multiple_of(k * SH, SH), SH)
        feat_a[:, cols] = features_a(tgt[k, 0:16, :])
        xt[:, cols] = tgt[k, 16:32, :]

    take_target(0)

    def next_target(k):
        arrived(k, tgt, tgt_rs)
        take_target(k)

    each(1, nc, next_target)

    def images_chunk(c):
        @pl.when(c != own // 2)
        def _():
            arrived(2 * c, src, src_rs)

        arrived(2 * c + 1, src, src_rs)
        one, two = src[2 * c], src[2 * c + 1]
        b = features_b(jnp.concatenate([one[0:16], two[0:16]], axis=1))
        x = jnp.concatenate([one[16:32], two[16:32]], axis=1)
        g = pair_values(jnp.dot(b, feat_a[...], preferred_element_type=F32))
        acc[...] += jnp.dot(x, g, preferred_element_type=F32)
        back = lax.dot_general(xt[...], g, over_lanes, preferred_element_type=F32).astype(BF16)
        rsr_out[2 * c] = back[:, 0:SH]
        rsr_out[2 * c + 1] = back[:, SH:2 * SH]
        for k in two_way:
            @pl.when(c == k // 2)
            def _():
                row_copy(order[k], k, rsr_out.at[k], rsr_in.at[k], rsr_ss, rsr_rs).start()

    each(0, chunks, images_chunk)

    def rs_send(k):
        rs_out[k] = acc[:, pl.ds(pl.multiple_of(k * SH, SH), SH)].astype(BF16)
        pltpu.make_async_remote_copy(
            src_ref=rs_out.at[k], dst_ref=rs_in.at[k], send_sem=rs_ss.at[k], recv_sem=rs_rs.at[k],
            device_id=(i, lax.rem(j + nc - k, nc)), device_id_type=MESH,
        ).start()

    each(1, nc, rs_send)

    each(0, nr - 1, lambda k: arrived(k, fpk, fpk_rs))
    packets = fpk[...].reshape(nr, 128)
    quarter = lax.broadcasted_iota(jnp.int32, (nz, 128), 1) // FD
    comps = []
    for c in range(4):
        comp = jnp.zeros((nz, 128), F32)
        for a in range(ny):
            moved = packets[a * nz:(a + 1) * nz]
            if a != c:
                moved = pltpu.roll(moved, FD * (a - c) % 128, 1)
            comp = jnp.where(quarter == a, moved, comp)
        comps.append(comp)
    frows = pieces([comp * CYCLES for comp in comps[:3]])
    detectors = lax.broadcasted_iota(jnp.int32, (GROUPS, 128), 0).astype(F32)
    for m in range(nz):
        for n, part in enumerate(frows):
            fgeo[m, n:n + 1, :] = part[m:m + 1]
        fgeo[m, 13:16, :] = jnp.zeros((3, 128), F32)
        onehot[:, m * 128:(m + 1) * 128] = (detectors == comps[3][m:m + 1]).astype(BF16)

    def field_chunk(c):
        b = features_b(jnp.concatenate([fgeo[2 * c], fgeo[2 * c + 1]], axis=1).astype(BF16))
        g = pair_values(jnp.dot(b, feat_a[...], preferred_element_type=F32))
        for q in range(nc // 2):
            gf[q, pl.ds(pl.multiple_of(c * 256, 256), 256), :] = g[:, q * 256:(q + 1) * 256]

    early = nz // 4
    each(0, early, field_chunk)

    rs_in[0] = jnp.zeros((WV, SH), BF16)
    total = acc[:, 0:SH]
    each(1, nc, lambda k: arrived(k, rs_in, rs_rs))
    total = total + jnp.sum(rs_in[...].astype(F32), axis=0)
    for k in two_way:
        arrived(k, rsr_in, rsr_rs)
        total = total + rsr_in[k].astype(F32)
    residual = inc[...] - self_term[...] * start - total * scale
    density = start + damping * precondition(residual)
    den_o[...] = density
    den[0] = (density * weight[...]).astype(BF16)
    each(1, nc, lambda k: col_copy(k, den.at[0], den.at[k], den_ss, den_rs).start())

    each(early, nz // 2, field_chunk)
    facc[...] = jnp.zeros_like(facc)

    def field_sum(q):
        @pl.when(q > 0)
        def _():
            arrived(2 * q, den, den_rs)

        arrived(2 * q + 1, den, den_rs)
        x = jnp.concatenate([den[2 * q], den[2 * q + 1]], axis=1)
        facc[...] += lax.dot_general(x, gf[q], over_lanes, preferred_element_type=F32)

    each(0, nc // 2, field_sum)

    fsum = facc[...] * scale
    h, m, l = split3(fsum)
    parts = jnp.concatenate([h.astype(BF16), m.astype(BF16), l.astype(BF16)], axis=0)
    sums = lax.dot_general(parts, onehot[...], over_lanes, preferred_element_type=F32)
    det1[j] = sums[0:WV] + sums[WV:2 * WV] + sums[2 * WV:3 * WV]
    each(1, nc, lambda k: col_copy(k, det1.at[j], det1.at[j], d1_ss, d1_rs).start())

    for m in range(nz):
        pot_out[m] = fsum[:, m * 128:(m + 1) * 128].astype(BF16)
    for k, d in enumerate(others):
        row_copy(d, k, pot_out.at[lax.rem(iz + d[0], nz)], pot_in.at[k], pot_ss, pot_rs).start()

    each(1, nc, lambda k: arrived(k, det1, d1_rs))
    det2[i] = jnp.sum(det1[...], axis=0)
    for k, d in enumerate(others):
        row_copy(d, k, det2.at[i], det2.at[i], d2_ss, d2_rs).start()

    each(0, nr - 1, lambda k: arrived(k, pot_in, pot_rs))
    pot_in[nr - 1] = pot_out[iz]
    pot = jnp.sum(pot_in[...].astype(F32), axis=0)
    pot = pltpu.roll(pot, lax.rem(128 - FD * iy, 128), 1)
    pot_o[...] = pot[:, 0:FD].astype(BF16)

    each(0, nr - 1, lambda k: arrived(k, det2, d2_rs))
    det_o[...] = jnp.sum(det2[...], axis=0) * wave_scale

    def sent(ks, buf, ss):
        def wait(k):
            pltpu.make_async_remote_copy(
                src_ref=buf.at[0], dst_ref=buf.at[0], send_sem=ss.at[k], recv_sem=ss.at[k],
                device_id=(i, j), device_id_type=MESH,
            ).wait_send()

        if isinstance(ks, range):
            each(ks.start, ks.stop, wait)
        else:
            for k in ks:
                wait(k)

    sent(range(1, nc), tgt, tgt_ss)
    sent(range(0, own), src, src_ss)
    sent(range(own + 1, len(order)), src, src_ss)
    sent(range(0, nr - 1), fpk, fpk_ss)
    sent(two_way, rsr_out, rsr_ss)
    sent(range(1, nc), rs_out, rs_ss)
    sent(range(1, nc), den, den_ss)
    sent(range(0, nr - 1), pot_out, pot_ss)
    sent(range(1, nc), det1, d1_ss)
    sent(range(0, nr - 1), det2, d2_ss)


def plan(nz, ny):
    def hops(d):
        return min(d[0], nz - d[0]) + 2 * min(d[1], ny - d[1])

    both = [(dz, dy) for dy in range(1, ny // 2) for dz in range(nz)]
    both += [(dz, dy) for dy in (0, ny // 2) for dz in range(1, nz // 2)]
    both = sorted(both, key=hops)
    pairs = [both[n:n + 2] for n in range(0, len(both), 2)]
    near = pairs[:len(pairs) // 2]
    far = pairs[len(pairs) // 2:][::-1]
    home = [(0, 0), (0, ny // 2)]
    last = [(nz // 2, 0), (nz // 2, ny // 2)]
    seq = near[:1] + [home] + near[1:] + far + [last]
    order = [d for pair in seq for d in pair]
    two_way = [k for k, d in enumerate(order) if d in both]
    return order, two_way, order.index((0, 0))


def local(
    nz, ny, nc, panel_xyz, panel_weight, self_term, panel_slot, block_inverse, incident, field_xyz, field_group
):
    nr = nz * ny
    panels = SH * nr * nc
    fields = field_xyz.shape[1]
    mine = nz * 128
    scale = CYCLES * B3 / math.sqrt(panels)
    wave_scale = 1.0 / math.sqrt(fields * nr / GROUPS)
    sel_b, sel_a = selectors()
    slots = len(plan(nz, ny)[0])
    vmem, dma = pltpu.VMEM, pltpu.SemaphoreType.DMA
    sems = [dma((10,))]
    for n in (slots, nc, slots, nc, nc, nr, nr, nc, nr):
        sems += [dma((n,)), dma((n,))]
    args = (
        panel_xyz, panel_weight, self_term.reshape(1, SH), panel_slot.reshape(1, SH), block_inverse, incident,
        field_xyz, field_group.reshape(1, FD), jnp.asarray(sel_b, BF16), jnp.asarray(sel_a, BF16),
    )
    return pl.pallas_call(
        functools.partial(kernel, nz, ny, nc, scale, wave_scale),
        out_shape=(
            jax.ShapeDtypeStruct((WV, SH), F32),
            jax.ShapeDtypeStruct((WV, FD), BF16),
            jax.ShapeDtypeStruct((WV, GROUPS), F32),
        ),
        in_specs=[pl.BlockSpec(memory_space=pltpu.HBM)] * 10,
        out_specs=(pl.BlockSpec(memory_space=pltpu.VMEM),) * 3,
        scratch_shapes=[vmem(a.shape, a.dtype) for a in args] + [
            vmem((16, SH), F32),
            vmem((2, 8, 128), F32),
            vmem((slots, 32, SH), BF16),
            vmem((nc, 32, SH), BF16),
            vmem((32, nc * SH), BF16),
            vmem((WV, nc * SH), BF16),
            vmem((SH, SH), F32),
            vmem((WV, nc * SH), F32),
            vmem((slots, WV, SH), BF16),
            vmem((slots, WV, SH), BF16),
            vmem((nc, WV, SH), BF16),
            vmem((nc, WV, SH), BF16),
            vmem((nr, 1, 128), F32),
            vmem((nz, 16, 128), F32),
            vmem((GROUPS, mine), BF16),
            vmem((nc, WV, SH), BF16),
            vmem((nc // 2, mine, 256), BF16),
            vmem((WV, mine), F32),
            vmem((nz, WV, 128), BF16),
            vmem((nr, WV, 128), BF16),
            vmem((nc, WV, GROUPS), F32),
            vmem((nr, WV, GROUPS), F32),
        ] + sems,
        compiler_params=pltpu.CompilerParams(
            collective_id=0, has_side_effects=True, vmem_limit_bytes=48 * 1024 * 1024
        ),
    )(*args)


def solution(mesh):
    nr, nc = mesh.shape["row"], mesh.shape["col"]
    ny = 4
    return jax.shard_map(
        functools.partial(local, nr // ny, ny, nc),
        mesh=mesh,
        in_specs=(
            P(None, ("col", "row")),
            P(None, ("col", "row")),
            P(("col", "row")),
            P(("col", "row")),
            P(None, ("col", "row")),
            P(None, ("col", "row")),
            P(None, "row"),
            P(("row", "col")),
        ),
        out_specs=(P(None, ("col", "row")), P(None, ("row", "col")), P()),
        check_vma=False,
    )
```

time: 93.7 us -> 79.1 us (0.84)
  Pallas kernels: 86 us -> 71.4 us
    pallas_call x1, Pallas kernels: 86 us -> 71.4 us  [local(): pl.pallas_call(functools.partial(kernel, nz, ny, nc, scale, wave_scale),...]
where the time goes in v2:
time: 79.1 us; the launch traced here: 78.7 us
  Pallas kernels  71.4 us (90%)
  local copies, waits for them, and re-layouts  6.65 us (8%)
    pallas_call x1, Pallas kernels, local(): pl.pallas_call(functools.partial(kernel, nz, ny, nc, scale, wave_scale),...  71.4 us
    unnamed x23, local copies, waits for them, and re-layouts  6.65 us

profile of v2, /device:TPU:1, one launch (start us, length us, event | category | flops | bytes accessed | tf_op | source)
XLA Modules:
  0.0 78.7 jit_solution(4840520313575490313)
XLA Ops:
  0.6 0.0 copy-start.4
  0.6 0.0 copy-start.6
  0.7 0.0 copy-start.7
  0.7 0.0 copy-start.8
  0.7 0.6 copy-done.4
  1.3 0.0 copy-done.6
  1.3 0.0 copy-done.7
  1.3 0.0 copy-done.8
  1.3 0.0 copy-start
  1.3 0.8 copy-done
  2.1 0.0 copy-start.1
  2.1 0.7 copy-done.1
  2.8 0.0 copy-start.2
  2.8 0.7 copy-done.2
  3.5 0.0 copy-start.3
  3.5 0.7 copy-done.3
  4.2 0.0 copy-start.5
  4.2 0.7 copy-done.5
  4.9 0.0 copy-start.9
  4.9 0.7 copy-done.9
  5.5 71.4 %shard_map.121 = (f32[16,128]{1,0:T(8,128)S(1)}, bf16[16,32]{1,0:T(8,128)(2,1)S(1)}, f32[16,128]{1,0:T(8,128)S(1)}) custom-call(f32[3,128]{1,0:T(4,128)S(1)} %copy-done.5, f32[1,128]{1,0:T(1,128)S(1)} %copy-done.6, f32[1,128]{1,0:T(1,128)S(1)} %bitcast.3, s32[1,128]{1,0:T(1,128)S(1)} %bitcast.4, f32[64,128]{1,0:T(8,128)S(1)} %copy-done, ...), custom_call_target="tpu_custom_call" | custom-call | tf_op jit(solution)/shard_map/pallas_call | solution.py:377
  76.9 0.6 copy.16
  77.5 0.6 copy.17
  78.1 0.6 copy.18
Async XLA Ops:
  0.6 0.7 copy-start.4
  0.6 0.7 copy-start.6
  0.7 0.7 copy-start.7
  0.7 0.7 copy-start.8
  1.3 0.8 copy-start
  2.1 0.7 copy-start.1
  2.8 0.7 copy-start.2
  3.5 0.7 copy-start.3
  4.2 0.7 copy-start.5
  4.9 0.7 copy-start.9

commit v3 on v2

--- a/solution.py
+++ b/solution.py
@@ -76,10 +76,10 @@
     xyz_h, weight_h, self_h, slot_h, binv_h, inc_h, fxyz_h, fgroup_h, sel_b_h, sel_a_h,
     den_o, pot_o, det_o,
     xyz, weight, self_term, slot, binv, inc, fxyz, fgroup, sel_b, sel_a,
-    geo_s, fs, src, tgt, feat_a, xt, coupled, acc, rsr_out, rsr_in, rs_out, rs_in, fpk, fgeo, onehot,
-    den, gf, facc, pot_out, pot_in, det1, det2,
+    geo_s, fs, src, tgt, feat_a, xt, coupled, acc, gbuf, rsr_out, rsr_in, rs_out, rs_in, fpk, fgeo, onehot,
+    den, gf, facc, pot_out, pot_in, detp, det1, det2, det3,
     load_s, src_ss, src_rs, tgt_ss, tgt_rs, rsr_ss, rsr_rs, rs_ss, rs_rs, den_ss, den_rs, fpk_ss, fpk_rs,
-    pot_ss, pot_rs, d1_ss, d1_rs, d2_ss, d2_rs,
+    pot_ss, pot_rs, d1_ss, d1_rs, d2_ss, d2_rs, d3_s,
 ):
     nr = nz * ny
     i = lax.axis_index("row")
@@ -187,39 +187,44 @@
 
     acc[...] = jnp.zeros_like(acc)
 
-    def take_target(k):
-        cols = pl.ds(pl.multiple_of(k * SH, SH), SH)
-        feat_a[:, cols] = features_a(tgt[k, 0:16, :])
-        xt[:, cols] = tgt[k, 16:32, :]
-
-    take_target(0)
-
-    def next_target(k):
-        arrived(k, tgt, tgt_rs)
-        take_target(k)
-
-    each(1, nc, next_target)
-
-    def images_chunk(c):
-        @pl.when(c != own // 2)
-        def _():
-            arrived(2 * c, src, src_rs)
-
-        arrived(2 * c + 1, src, src_rs)
-        one, two = src[2 * c], src[2 * c + 1]
-        b = features_b(jnp.concatenate([one[0:16], two[0:16]], axis=1))
-        x = jnp.concatenate([one[16:32], two[16:32]], axis=1)
-        g = pair_values(jnp.dot(b, feat_a[...], preferred_element_type=F32))
+    each(1, nc, lambda k: arrived(k, tgt, tgt_rs))
+    for k in range(0, nc, 4):
+        group = [tgt[n] for n in range(k, k + 4)]
+        feat_a[:, k * SH:(k + 4) * SH] = features_a(jnp.concatenate([p[0:16] for p in group], axis=1))
+        xt[:, k * SH:(k + 4) * SH] = jnp.concatenate([p[16:32] for p in group], axis=1)
+
+    def tile(c):
+        b = features_b(jnp.concatenate([src[2 * c, 0:16, :], src[2 * c + 1, 0:16, :]], axis=1))
+        gbuf[...] = pair_values(jnp.dot(b, feat_a[...], preferred_element_type=F32))
+
+    def use(c):
+        x = jnp.concatenate([src[2 * c, 16:32, :], src[2 * c + 1, 16:32, :]], axis=1)
+        g = gbuf[...]
         acc[...] += jnp.dot(x, g, preferred_element_type=F32)
         back = lax.dot_general(xt[...], g, over_lanes, preferred_element_type=F32).astype(BF16)
         rsr_out[2 * c] = back[:, 0:SH]
         rsr_out[2 * c + 1] = back[:, SH:2 * SH]
+
+    def wait_chunk(c):
+        @pl.when(c != own // 2)
+        def _():
+            arrived(2 * c, src, src_rs)
+
+        arrived(2 * c + 1, src, src_rs)
+
+    def images_chunk(c):
+        wait_chunk(c)
+        use(c - 1)
+        tile(c)
         for k in two_way:
-            @pl.when(c == k // 2)
+            @pl.when(c - 1 == k // 2)
             def _():
                 row_copy(order[k], k, rsr_out.at[k], rsr_in.at[k], rsr_ss, rsr_rs).start()
 
-    each(0, chunks, images_chunk)
+    wait_chunk(0)
+    tile(0)
+    each(1, chunks, images_chunk)
+    use(chunks - 1)
 
     def rs_send(k):
         rs_out[k] = acc[:, pl.ds(pl.multiple_of(k * SH, SH), SH)].astype(BF16)
@@ -290,8 +295,13 @@
     h, m, l = split3(fsum)
     parts = jnp.concatenate([h.astype(BF16), m.astype(BF16), l.astype(BF16)], axis=0)
     sums = lax.dot_general(parts, onehot[...], over_lanes, preferred_element_type=F32)
-    det1[j] = sums[0:WV] + sums[WV:2 * WV] + sums[2 * WV:3 * WV]
-    each(1, nc, lambda k: col_copy(k, det1.at[j], det1.at[j], d1_ss, d1_rs).start())
+    detp[...] = sums[0:WV] + sums[WV:2 * WV] + sums[2 * WV:3 * WV]
+
+    def waves_of(col):
+        return pl.ds(pl.multiple_of(lax.rem(col, 2) * 8, 8), 8)
+
+    each(1, nc, lambda k: col_copy(k, detp.at[waves_of(j + k)], det1.at[j], d1_ss, d1_rs).start())
+    det1[j] = detp[waves_of(j), :]
 
     for m in range(nz):
         pot_out[m] = fsum[:, m * 128:(m + 1) * 128].astype(BF16)
@@ -310,7 +320,15 @@
     pot_o[...] = pot[:, 0:FD].astype(BF16)
 
     each(0, nr - 1, lambda k: arrived(k, det2, d2_rs))
-    det_o[...] = jnp.sum(det2[...], axis=0) * wave_scale
+    core = lax.rem(j, 2)
+    det3[core] = jnp.sum(det2[...], axis=0) * wave_scale
+    swap = pltpu.make_async_remote_copy(
+        src_ref=det3.at[core], dst_ref=det3.at[core], send_sem=d3_s.at[0], recv_sem=d3_s.at[1],
+        device_id=(i, j + 1 - 2 * core), device_id_type=MESH,
+    )
+    swap.start()
+    swap.wait()
+    det_o[...] = jnp.concatenate([det3[0], det3[1]], axis=0)
 
     def sent(ks, buf, ss):
         def wait(k):
@@ -370,6 +388,7 @@
     sems = [dma((10,))]
     for n in (slots, nc, slots, nc, nc, nr, nr, nc, nr):
         sems += [dma((n,)), dma((n,))]
+    sems += [dma((2,))]
     args = (
         panel_xyz, panel_weight, self_term.reshape(1, SH), panel_slot.reshape(1, SH), block_inverse, incident,
         field_xyz, field_group.reshape(1, FD), jnp.asarray(sel_b, BF16), jnp.asarray(sel_a, BF16),
@@ -392,6 +411,7 @@
             vmem((WV, nc * SH), BF16),
             vmem((SH, SH), F32),
             vmem((WV, nc * SH), F32),
+            vmem((2 * SH, nc * SH), BF16),
             vmem((slots, WV, SH), BF16),
             vmem((slots, WV, SH), BF16),
             vmem((nc, WV, SH), BF16),
@@ -404,11 +424,13 @@
             vmem((WV, mine), F32),
             vmem((nz, WV, 128), BF16),
             vmem((nr, WV, 128), BF16),
-            vmem((nc, WV, GROUPS), F32),
-            vmem((nr, WV, GROUPS), F32),
+            vmem((WV, GROUPS), F32),
+            vmem((nc, 8, GROUPS), F32),
+            vmem((nr, 8, GROUPS), F32),
+            vmem((2, 8, GROUPS), F32),
         ] + sems,
         compiler_params=pltpu.CompilerParams(
-            collective_id=0, has_side_effects=True, vmem_limit_bytes=48 * 1024 * 1024
+            collective_id=0, has_side_effects=True, vmem_limit_bytes=67043328
         ),
     )(*args)
 

time: 79.1 us -> 75.5 us (0.954)
  local copies, waits for them, and re-layouts: 6.65 us -> 2.6 us
    unnamed x23 -> x7, local copies, waits for them, and re-layouts: 6.65 us -> 2.6 us
where the time goes in v3:
time: 75.5 us; the launch traced here: 75.2 us
  Pallas kernels  71.9 us (95%)
  local copies, waits for them, and re-layouts  2.6 us (3%)
    pallas_call x1, Pallas kernels, local(): pl.pallas_call(functools.partial(kernel, nz, ny, nc, scale, wave_scale),...  71.9 us
    unnamed x7, local copies, waits for them, and re-layouts  2.6 us

profile of v3, /device:TPU:1, one launch (start us, length us, event | category | flops | bytes accessed | tf_op | source)
XLA Modules:
  0.0 75.2 jit_solution(2690506746057881722)
XLA Ops:
  0.6 71.9 %shard_map.121 = (f32[16,128]{1,0:T(8,128)}, bf16[16,32]{1,0:T(8,128)(2,1)}, f32[16,128]{1,0:T(8,128)}) custom-call(f32[3,128]{1,0:T(4,128)} %xyz_h.1, f32[1,128]{1,0:T(1,128)} %weight_h.1, f32[1,128]{1,0:T(1,128)} %bitcast.3, s32[1,128]{1,0:T(1,128)} %bitcast.4, f32[64,128]{1,0:T(8,128)} %binv_h.1, f32[16,128]{1,0:T(8,128)} %inc_h.1, f32[3,512]{1,0:T(4,128)} %fxyz_h.1, ...), custom_call_target="tpu_custom_call" | custom-call | tf_op jit(solution)/shard_map/pallas_call | solution.py:396
  72.6 0.0 copy-start.1
  72.6 1.3 %copy.16 = f32[16,128]{1,0:T(8,128)} copy(f32[16,128]{1,0:T(8,128)} %get-tuple-element.6) | data formatting | bytes 16384
  73.9 0.0 copy-done.1
  73.9 0.0 copy-start
  73.9 0.6 copy.17
  74.5 0.1 copy-done
  74.6 0.6 copy.18
Async XLA Ops:
  72.6 1.3 %copy-start.1 = (bf16[16,32]{1,0:T(8,128)(2,1)S(1)}, bf16[16,32]{1,0:T(8,128)(2,1)}, u32[]{:S(2)}) copy-start(bf16[16,32]{1,0:T(8,128)(2,1)} %get-tuple-element.7) | copy-start | bytes 3076
  73.9 0.7 copy-start

commit v4 on v3

--- a/solution.py
+++ b/solution.py
@@ -22,7 +22,7 @@
 smoothing = 0.05
 damping = 0.5
 
-B0, B1, B2, B3 = 6.283164041181243, -41.33714186520903, 81.3407492682057, -70.99322232997507
+LEAD, A1, A0 = 73.90290388562806, -0.5546875, 0.0849609375
 CYCLES = wave_number / (2.0 * math.pi)
 EPS = smoothing * smoothing * CYCLES * CYCLES
 
@@ -65,10 +65,10 @@
 def pair_values(d):
     s = jnp.maximum(d, 1e-12)
     r = s * lax.rsqrt(s)
-    v = 0.25 - jnp.abs(r - jnp.round(r))
+    v = (0.25 - jnp.abs(r - jnp.round(r))).astype(BF16)
     q = v * v
-    p = ((q + B2 / B3) * q + B1 / B3) * q + B0 / B3
-    return ((p * v) * lax.rsqrt(s + EPS)).astype(BF16)
+    p = (q + BF16(A1)) * q + BF16(A0)
+    return (p * v) * lax.rsqrt(s + EPS).astype(BF16)
 
 
 def kernel(
@@ -76,9 +76,9 @@
     xyz_h, weight_h, self_h, slot_h, binv_h, inc_h, fxyz_h, fgroup_h, sel_b_h, sel_a_h,
     den_o, pot_o, det_o,
     xyz, weight, self_term, slot, binv, inc, fxyz, fgroup, sel_b, sel_a,
-    geo_s, fs, src, tgt, feat_a, xt, coupled, acc, gbuf, rsr_out, rsr_in, rs_out, rs_in, fpk, fgeo, onehot,
+    geo_s, fs, src, tgt, tgx, feat_a, feat_b, feat_f, xt, coupled, acc, gbuf, rsr_out, rsr_in, rs_out, rs_in, fpk, fgeo, onehot,
     den, gf, facc, pot_out, pot_in, detp, det1, det2, det3,
-    load_s, src_ss, src_rs, tgt_ss, tgt_rs, rsr_ss, rsr_rs, rs_ss, rs_rs, den_ss, den_rs, fpk_ss, fpk_rs,
+    load_s, src_ss, src_rs, tgt_ss, tgt_rs, tgx_ss, tgx_rs, rsr_ss, rsr_rs, rs_ss, rs_rs, den_ss, den_rs, fpk_ss, fpk_rs,
     pot_ss, pot_rs, d1_ss, d1_rs, d2_ss, d2_rs, d3_s,
 ):
     nr = nz * ny
@@ -119,7 +119,7 @@
     geo_s[13:16, :] = jnp.zeros((3, SH), F32)
     packet = geo_s[...].astype(BF16)
     src[own, 0:16, :] = packet
-    tgt[0, 0:16, :] = packet
+    tgt[0] = packet
     place = lax.broadcasted_iota(jnp.int32, (64, SH), 0)
     chosen = (place == slot[...] % 64).astype(F32)
     half = (lax.broadcasted_iota(jnp.int32, (8, SH), 0) == slot[...] // 64).astype(F32)
@@ -136,7 +136,7 @@
     start = precondition(inc[...])
     start_w = (start * weight[...]).astype(BF16)
     src[own, 16:32, :] = start_w
-    tgt[0, 16:32, :] = start_w
+    tgx[0] = start_w
 
     lane = lax.broadcasted_iota(jnp.int32, (8, 128), 1)
     fs[...] = jnp.zeros_like(fs)
@@ -173,6 +173,8 @@
 
     each(1, nc, lambda k: col_copy(k, tgt.at[0], tgt.at[k], tgt_ss, tgt_rs).start())
     for k, (dz, dy) in enumerate(order):
+        if k == 4:
+            each(1, nc, lambda n: col_copy(n, tgx.at[0], tgx.at[n], tgx_ss, tgx_rs).start())
         if k != own:
             row_copy((-dz, -dy), k, src.at[own], src.at[k], src_ss, src_rs).start()
     others = [(dz, dy) for dz in range(nz) for dy in range(ny)][1:]
@@ -189,13 +191,13 @@
 
     each(1, nc, lambda k: arrived(k, tgt, tgt_rs))
     for k in range(0, nc, 4):
-        group = [tgt[n] for n in range(k, k + 4)]
-        feat_a[:, k * SH:(k + 4) * SH] = features_a(jnp.concatenate([p[0:16] for p in group], axis=1))
-        xt[:, k * SH:(k + 4) * SH] = jnp.concatenate([p[16:32] for p in group], axis=1)
-
-    def tile(c):
-        b = features_b(jnp.concatenate([src[2 * c, 0:16, :], src[2 * c + 1, 0:16, :]], axis=1))
-        gbuf[...] = pair_values(jnp.dot(b, feat_a[...], preferred_element_type=F32))
+        feat_a[:, k * SH:(k + 4) * SH] = features_a(jnp.concatenate([tgt[n] for n in range(k, k + 4)], axis=1))
+
+    def tile(b):
+        return pair_values(jnp.dot(b, feat_a[...], preferred_element_type=F32))
+
+    def source_features(c):
+        return features_b(jnp.concatenate([src[2 * c, 0:16, :], src[2 * c + 1, 0:16, :]], axis=1))
 
     def use(c):
         x = jnp.concatenate([src[2 * c, 16:32, :], src[2 * c + 1, 16:32, :]], axis=1)
@@ -213,16 +215,26 @@
         arrived(2 * c + 1, src, src_rs)
 
     def images_chunk(c):
-        wait_chunk(c)
+        @pl.when(c + 1 < chunks)
+        def _():
+            wait_chunk(c + 1)
+
+        b = feat_b[...]
         use(c - 1)
-        tile(c)
+        gbuf[...] = tile(b)
+        feat_b[...] = source_features(jnp.minimum(c + 1, chunks - 1))
         for k in two_way:
             @pl.when(c - 1 == k // 2)
             def _():
                 row_copy(order[k], k, rsr_out.at[k], rsr_in.at[k], rsr_ss, rsr_rs).start()
 
     wait_chunk(0)
-    tile(0)
+    wait_chunk(1)
+    gbuf[...] = tile(source_features(0))
+    feat_b[...] = source_features(1)
+    each(1, nc, lambda k: arrived(k, tgx, tgx_rs))
+    for k in range(nc):
+        xt[:, k * SH:(k + 1) * SH] = tgx[k]
     each(1, chunks, images_chunk)
     use(chunks - 1)
 
@@ -255,9 +267,12 @@
         fgeo[m, 13:16, :] = jnp.zeros((3, 128), F32)
         onehot[:, m * 128:(m + 1) * 128] = (detectors == comps[3][m:m + 1]).astype(BF16)
 
+    for c in range(nz // 2):
+        feat_f[c * 256:(c + 1) * 256, :] = features_b(
+            jnp.concatenate([fgeo[2 * c], fgeo[2 * c + 1]], axis=1).astype(BF16))
+
     def field_chunk(c):
-        b = features_b(jnp.concatenate([fgeo[2 * c], fgeo[2 * c + 1]], axis=1).astype(BF16))
-        g = pair_values(jnp.dot(b, feat_a[...], preferred_element_type=F32))
+        g = tile(feat_f[pl.ds(pl.multiple_of(c * 256, 256), 256), :])
         for q in range(nc // 2):
             gf[q, pl.ds(pl.multiple_of(c * 256, 256), 256), :] = g[:, q * 256:(q + 1) * 256]
 
@@ -344,6 +359,7 @@
                 wait(k)
 
     sent(range(1, nc), tgt, tgt_ss)
+    sent(range(1, nc), tgx, tgx_ss)
     sent(range(0, own), src, src_ss)
     sent(range(own + 1, len(order)), src, src_ss)
     sent(range(0, nr - 1), fpk, fpk_ss)
@@ -380,13 +396,13 @@
     panels = SH * nr * nc
     fields = field_xyz.shape[1]
     mine = nz * 128
-    scale = CYCLES * B3 / math.sqrt(panels)
+    scale = CYCLES * LEAD / math.sqrt(panels)
     wave_scale = 1.0 / math.sqrt(fields * nr / GROUPS)
     sel_b, sel_a = selectors()
     slots = len(plan(nz, ny)[0])
     vmem, dma = pltpu.VMEM, pltpu.SemaphoreType.DMA
     sems = [dma((10,))]
-    for n in (slots, nc, slots, nc, nc, nr, nr, nc, nr):
+    for n in (slots, nc, nc, slots, nc, nc, nr, nr, nc, nr):
         sems += [dma((n,)), dma((n,))]
     sems += [dma((2,))]
     args = (
@@ -406,8 +422,11 @@
             vmem((16, SH), F32),
             vmem((2, 8, 128), F32),
             vmem((slots, 32, SH), BF16),
-            vmem((nc, 32, SH), BF16),
+            vmem((nc, 16, SH), BF16),
+            vmem((nc, WV, SH), BF16),
             vmem((32, nc * SH), BF16),
+            vmem((2 * SH, 32), BF16),
+            vmem((mine, 32), BF16),
             vmem((WV, nc * SH), BF16),
             vmem((SH, SH), F32),
             vmem((WV, nc * SH), F32),

time: 75.5 us -> 68.6 us (0.909)
  Pallas kernels: 71.9 us -> 65.1 us
    pallas_call x1, Pallas kernels: 71.9 us -> 65.1 us  [local(): pl.pallas_call(functools.partial(kernel, nz, ny, nc, scale, wave_scale),...]
where the time goes in v4:
time: 68.6 us; the launch traced here: 68.3 us
  Pallas kernels  65.1 us (95%)
  local copies, waits for them, and re-layouts  2.6 us (4%)
    pallas_call x1, Pallas kernels, local(): pl.pallas_call(functools.partial(kernel, nz, ny, nc, scale, wave_scale),...  65.1 us
    unnamed x7, local copies, waits for them, and re-layouts  2.6 us

profile of v4, /device:TPU:1, one launch (start us, length us, event | category | flops | bytes accessed | tf_op | source)
XLA Modules:
  0.0 68.3 jit_solution(16621786804759366708)
XLA Ops:
  0.6 65.1 %shard_map.121 = (f32[16,128]{1,0:T(8,128)}, bf16[16,32]{1,0:T(8,128)(2,1)}, f32[16,128]{1,0:T(8,128)}) custom-call(f32[3,128]{1,0:T(4,128)} %xyz_h.1, f32[1,128]{1,0:T(1,128)} %weight_h.1, f32[1,128]{1,0:T(1,128)} %bitcast.3, s32[1,128]{1,0:T(1,128)} %bitcast.4, f32[64,128]{1,0:T(8,128)} %binv_h.1, f32[16,128]{1,0:T(8,128)} %inc_h.1, f32[3,512]{1,0:T(4,128)} %fxyz_h.1, ...), custom_call_target="tpu_custom_call" | custom-call | tf_op jit(solution)/shard_map/pallas_call | solution.py:412
  65.7 0.0 copy-start.1
  65.7 1.3 %copy.16 = f32[16,128]{1,0:T(8,128)} copy(f32[16,128]{1,0:T(8,128)} %get-tuple-element.6) | data formatting | bytes 16384
  67.0 0.0 copy-done.1
  67.0 0.0 copy-start
  67.0 0.6 copy.17
  67.6 0.1 copy-done
  67.7 0.6 copy.18
Async XLA Ops:
  65.7 1.3 %copy-start.1 = (bf16[16,32]{1,0:T(8,128)(2,1)S(1)}, bf16[16,32]{1,0:T(8,128)(2,1)}, u32[]{:S(2)}) copy-start(bf16[16,32]{1,0:T(8,128)(2,1)} %get-tuple-element.7) | copy-start | bytes 3076
  67.0 0.7 %copy-start = (f32[16,128]{1,0:T(8,128)S(1)}, f32[16,128]{1,0:T(8,128)}, u32[]{:S(2)}) copy-start(f32[16,128]{1,0:T(8,128)} %get-tuple-element.8) | copy-start | bytes 24580

commit v5 on v4

--- a/solution.py
+++ b/solution.py
@@ -77,7 +77,7 @@
     den_o, pot_o, det_o,
     xyz, weight, self_term, slot, binv, inc, fxyz, fgroup, sel_b, sel_a,
     geo_s, fs, src, tgt, tgx, feat_a, feat_b, feat_f, xt, coupled, acc, gbuf, rsr_out, rsr_in, rs_out, rs_in, fpk, fgeo, onehot,
-    den, gf, facc, pot_out, pot_in, detp, det1, det2, det3,
+    den, gf, pot_out, pot_in, detp, det1, det2, det3,
     load_s, src_ss, src_rs, tgt_ss, tgt_rs, tgx_ss, tgx_rs, rsr_ss, rsr_rs, rs_ss, rs_rs, den_ss, den_rs, fpk_ss, fpk_rs,
     pot_ss, pot_rs, d1_ss, d1_rs, d2_ss, d2_rs, d3_s,
 ):
@@ -96,8 +96,8 @@
         lax.fori_loop(lo, hi, step, 0)
 
     barrier = pltpu.get_barrier_semaphore()
-    each(1, nr, lambda n: pl.semaphore_signal(
-        barrier, inc=1, device_id=(lax.rem(i + n, nr), j), device_id_type=MESH))
+    each(0, nr - 1, lambda n: pl.semaphore_signal(
+        barrier, inc=1, device_id=(lax.rem(i + 1 + lax.rem(n + nr // 2 - 1, nr - 1), nr), j), device_id_type=MESH))
     each(1, nc, lambda n: pl.semaphore_signal(
         barrier, inc=1, device_id=(i, lax.rem(j + n, nc)), device_id_type=MESH))
 
@@ -177,7 +177,8 @@
             each(1, nc, lambda n: col_copy(n, tgx.at[0], tgx.at[n], tgx_ss, tgx_rs).start())
         if k != own:
             row_copy((-dz, -dy), k, src.at[own], src.at[k], src_ss, src_rs).start()
-    others = [(dz, dy) for dz in range(nz) for dy in range(ny)][1:]
+    others = sorted([(dz, dy) for dz in range(nz) for dy in range(ny)][1:],
+                    key=lambda d: -min(d[0], nz - d[0]) - 2 * min(d[1], ny - d[1]))
     for k, d in enumerate(others):
         row_copy(d, k, fpk.at[mine], fpk.at[mine], fpk_ss, fpk_rs).start()
 
@@ -273,8 +274,7 @@
 
     def field_chunk(c):
         g = tile(feat_f[pl.ds(pl.multiple_of(c * 256, 256), 256), :])
-        for q in range(nc // 2):
-            gf[q, pl.ds(pl.multiple_of(c * 256, 256), 256), :] = g[:, q * 256:(q + 1) * 256]
+        gf[pl.ds(pl.multiple_of(c * 256, 256), 256), :] = g
 
     early = nz // 4
     each(0, early, field_chunk)
@@ -293,20 +293,9 @@
     each(1, nc, lambda k: col_copy(k, den.at[0], den.at[k], den_ss, den_rs).start())
 
     each(early, nz // 2, field_chunk)
-    facc[...] = jnp.zeros_like(facc)
-
-    def field_sum(q):
-        @pl.when(q > 0)
-        def _():
-            arrived(2 * q, den, den_rs)
-
-        arrived(2 * q + 1, den, den_rs)
-        x = jnp.concatenate([den[2 * q], den[2 * q + 1]], axis=1)
-        facc[...] += lax.dot_general(x, gf[q], over_lanes, preferred_element_type=F32)
-
-    each(0, nc // 2, field_sum)
-
-    fsum = facc[...] * scale
+    each(1, nc, lambda k: arrived(k, den, den_rs))
+    x = jnp.concatenate([den[k] for k in range(nc)], axis=1)
+    fsum = lax.dot_general(x, gf[...], over_lanes, preferred_element_type=F32) * scale
     h, m, l = split3(fsum)
     parts = jnp.concatenate([h.astype(BF16), m.astype(BF16), l.astype(BF16)], axis=0)
     sums = lax.dot_general(parts, onehot[...], over_lanes, preferred_element_type=F32)
@@ -409,13 +398,15 @@
         panel_xyz, panel_weight, self_term.reshape(1, SH), panel_slot.reshape(1, SH), block_inverse, incident,
         field_xyz, field_group.reshape(1, FD), jnp.asarray(sel_b, BF16), jnp.asarray(sel_a, BF16),
     )
-    return pl.pallas_call(
+    shapes = (
+        jax.ShapeDtypeStruct((WV, SH), F32),
+        jax.ShapeDtypeStruct((WV, FD), BF16),
+        jax.ShapeDtypeStruct((WV, GROUPS), F32),
+    )
+    hbm = pl.BlockSpec(memory_space=pltpu.HBM)
+    results = pl.pallas_call(
         functools.partial(kernel, nz, ny, nc, scale, wave_scale),
-        out_shape=(
-            jax.ShapeDtypeStruct((WV, SH), F32),
-            jax.ShapeDtypeStruct((WV, FD), BF16),
-            jax.ShapeDtypeStruct((WV, GROUPS), F32),
-        ),
+        out_shape=shapes,
         in_specs=[pl.BlockSpec(memory_space=pltpu.HBM)] * 10,
         out_specs=(pl.BlockSpec(memory_space=pltpu.VMEM),) * 3,
         scratch_shapes=[vmem(a.shape, a.dtype) for a in args] + [
@@ -439,8 +430,7 @@
             vmem((nz, 16, 128), F32),
             vmem((GROUPS, mine), BF16),
             vmem((nc, WV, SH), BF16),
-            vmem((nc // 2, mine, 256), BF16),
-            vmem((WV, mine), F32),
+            vmem((mine, nc * SH), BF16),
             vmem((nz, WV, 128), BF16),
             vmem((nr, WV, 128), BF16),
             vmem((WV, GROUPS), F32),
@@ -452,6 +442,26 @@
             collective_id=0, has_side_effects=True, vmem_limit_bytes=67043328
         ),
     )(*args)
+    return pl.pallas_call(
+        hand_out,
+        out_shape=shapes,
+        in_specs=[hbm] * 3,
+        out_specs=(hbm,) * 3,
+        scratch_shapes=[vmem(a.shape, a.dtype) for a in shapes] + [dma((3,)), dma((3,))],
+        compiler_params=pltpu.CompilerParams(vmem_limit_bytes=67043328),
+    )(*results)
+
+
+def hand_out(a0, a1, a2, o0, o1, o2, s0, s1, s2, in_s, out_s):
+    taken = [pltpu.make_async_copy(a, s, in_s.at[n]) for n, (a, s) in enumerate(((a0, s0), (a1, s1), (a2, s2)))]
+    given = [pltpu.make_async_copy(s, o, out_s.at[n]) for n, (s, o) in enumerate(((s0, o0), (s1, o1), (s2, o2)))]
+    for copy in taken:
+        copy.start()
+    for copy, put in zip(taken, given):
+        copy.wait()
+        put.start()
+    for put in given:
+        put.wait()
 
 
 def solution(mesh):

time: 68.6 us -> 67 us (0.977)
  local copies, waits for them, and re-layouts: 2.6 us -> 0 us
  Pallas kernels: 65.1 us -> 66.1 us
    unnamed x7 -> x0, local copies, waits for them, and re-layouts: 2.6 us -> none
    pallas_call x0 -> x1, Pallas kernels: none -> 1.37 us  [local(): pl.pallas_call(hand_out, out_shape=shapes, in_specs=[hbm] * 3, out_specs=...]
where the time goes in v5:
time: 67 us; the launch traced here: 66.7 us
  Pallas kernels  66.1 us (99%)
    pallas_call x1, Pallas kernels, local(): pl.pallas_call(functools.partial(kernel, nz, ny, nc, scale, wave_scale),...  64.7 us
    pallas_call x1, Pallas kernels, local(): pl.pallas_call(hand_out, out_shape=shapes, in_specs=[hbm] * 3, out_specs=...  1.37 us

profile of v5, /device:TPU:1, one launch (start us, length us, event | category | flops | bytes accessed | tf_op | source)
XLA Modules:
  0.0 66.7 jit_solution(4868683404413393059)
XLA Ops:
  0.6 64.7 %shard_map.121 = (f32[16,128]{1,0:T(8,128)}, bf16[16,32]{1,0:T(8,128)(2,1)}, f32[16,128]{1,0:T(8,128)}) custom-call(f32[3,128]{1,0:T(4,128)} %xyz_h.1, f32[1,128]{1,0:T(1,128)} %weight_h.1, f32[1,128]{1,0:T(1,128)} %bitcast.3, s32[1,128]{1,0:T(1,128)} %bitcast.4, f32[64,128]{1,0:T(8,128)} %binv_h.1, f32[16,128]{1,0:T(8,128)} %inc_h.1, f32[3,512]{1,0:T(4,128)} %fxyz_h.1, ...), custom_call_target="tpu_custom_call" | custom-call | tf_op jit(solution)/shard_map/pallas_call | solution.py:407
  65.3 1.4 %shard_map.122 = (f32[16,128]{1,0:T(8,128)}, bf16[16,32]{1,0:T(8,128)(2,1)}, f32[16,128]{1,0:T(8,128)}) custom-call(f32[16,128]{1,0:T(8,128)} %get-tuple-element.6.a0, bf16[16,32]{1,0:T(8,128)(2,1)} %get-tuple-element.7.a1, f32[16,128]{1,0:T(8,128)} %get-tuple-element.8.a2), custom_call_target="tpu_custom_call" | custom-call | tf_op jit(solution)/shard_map/pallas_call | solution.py:445

commit v6 on v5

--- a/solution.py
+++ b/solution.py
@@ -77,7 +77,7 @@
     den_o, pot_o, det_o,
     xyz, weight, self_term, slot, binv, inc, fxyz, fgroup, sel_b, sel_a,
     geo_s, fs, src, tgt, tgx, feat_a, feat_b, feat_f, xt, coupled, acc, gbuf, rsr_out, rsr_in, rs_out, rs_in, fpk, fgeo, onehot,
-    den, gf, pot_out, pot_in, detp, det1, det2, det3,
+    den, gf, pot_out, pot_in, detp, det1, det2, detz, det3,
     load_s, src_ss, src_rs, tgt_ss, tgt_rs, tgx_ss, tgx_rs, rsr_ss, rsr_rs, rs_ss, rs_rs, den_ss, den_rs, fpk_ss, fpk_rs,
     pot_ss, pot_rs, d1_ss, d1_rs, d2_ss, d2_rs, d3_s,
 ):
@@ -190,20 +190,18 @@
 
     acc[...] = jnp.zeros_like(acc)
 
-    each(1, nc, lambda k: arrived(k, tgt, tgt_rs))
-    for k in range(0, nc, 4):
-        feat_a[:, k * SH:(k + 4) * SH] = features_a(jnp.concatenate([tgt[n] for n in range(k, k + 4)], axis=1))
-
     def tile(b):
         return pair_values(jnp.dot(b, feat_a[...], preferred_element_type=F32))
 
     def source_features(c):
         return features_b(jnp.concatenate([src[2 * c, 0:16, :], src[2 * c + 1, 0:16, :]], axis=1))
 
-    def use(c):
+    def use(c, last=False):
         x = jnp.concatenate([src[2 * c, 16:32, :], src[2 * c + 1, 16:32, :]], axis=1)
         g = gbuf[...]
         acc[...] += jnp.dot(x, g, preferred_element_type=F32)
+        if last:
+            return
         back = lax.dot_general(xt[...], g, over_lanes, preferred_element_type=F32).astype(BF16)
         rsr_out[2 * c] = back[:, 0:SH]
         rsr_out[2 * c + 1] = back[:, SH:2 * SH]
@@ -230,14 +228,18 @@
                 row_copy(order[k], k, rsr_out.at[k], rsr_in.at[k], rsr_ss, rsr_rs).start()
 
     wait_chunk(0)
+    first = source_features(0)
     wait_chunk(1)
-    gbuf[...] = tile(source_features(0))
     feat_b[...] = source_features(1)
+    each(1, nc, lambda k: arrived(k, tgt, tgt_rs))
+    for k in range(0, nc, 4):
+        feat_a[:, k * SH:(k + 4) * SH] = features_a(jnp.concatenate([tgt[n] for n in range(k, k + 4)], axis=1))
+    gbuf[...] = tile(first)
     each(1, nc, lambda k: arrived(k, tgx, tgx_rs))
     for k in range(nc):
         xt[:, k * SH:(k + 1) * SH] = tgx[k]
     each(1, chunks, images_chunk)
-    use(chunks - 1)
+    use(chunks - 1, last=True)
 
     def rs_send(k):
         rs_out[k] = acc[:, pl.ds(pl.multiple_of(k * SH, SH), SH)].astype(BF16)
@@ -313,9 +315,16 @@
         row_copy(d, k, pot_out.at[lax.rem(iz + d[0], nz)], pot_in.at[k], pot_ss, pot_rs).start()
 
     each(1, nc, lambda k: arrived(k, det1, d1_rs))
-    det2[i] = jnp.sum(det1[...], axis=0)
-    for k, d in enumerate(others):
-        row_copy(d, k, det2.at[i], det2.at[i], d2_ss, d2_rs).start()
+    det2[iy] = jnp.sum(det1[...], axis=0)
+    along_y = [(0, dy) for dy in (ny // 2, *[n for n in range(1, ny) if n != ny // 2])]
+    for k, d in enumerate(along_y):
+        row_copy(d, k, det2.at[iy], det2.at[iy], d2_ss, d2_rs).start()
+
+    for k in range(ny - 1):
+        arrived(k, det2, d2_rs)
+    detz[iz] = jnp.sum(det2[...], axis=0)
+    for dz in sorted(range(1, nz), key=lambda n: -min(n, nz - n)):
+        row_copy((dz, 0), ny - 1 + dz, detz.at[iz], detz.at[iz], d2_ss, d2_rs).start()
 
     each(0, nr - 1, lambda k: arrived(k, pot_in, pot_rs))
     pot_in[nr - 1] = pot_out[iz]
@@ -323,9 +332,9 @@
     pot = pltpu.roll(pot, lax.rem(128 - FD * iy, 128), 1)
     pot_o[...] = pot[:, 0:FD].astype(BF16)
 
-    each(0, nr - 1, lambda k: arrived(k, det2, d2_rs))
+    each(ny, ny + nz - 1, lambda k: arrived(k, detz, d2_rs))
     core = lax.rem(j, 2)
-    det3[core] = jnp.sum(det2[...], axis=0) * wave_scale
+    det3[core] = jnp.sum(detz[...], axis=0) * wave_scale
     swap = pltpu.make_async_remote_copy(
         src_ref=det3.at[core], dst_ref=det3.at[core], send_sem=d3_s.at[0], recv_sem=d3_s.at[1],
         device_id=(i, j + 1 - 2 * core), device_id_type=MESH,
@@ -357,7 +366,8 @@
     sent(range(1, nc), den, den_ss)
     sent(range(0, nr - 1), pot_out, pot_ss)
     sent(range(1, nc), det1, d1_ss)
-    sent(range(0, nr - 1), det2, d2_ss)
+    sent(range(0, ny - 1), det2, d2_ss)
+    sent(range(ny, ny + nz - 1), detz, d2_ss)
 
 
 def plan(nz, ny):
@@ -435,7 +445,8 @@
             vmem((nr, WV, 128), BF16),
             vmem((WV, GROUPS), F32),
             vmem((nc, 8, GROUPS), F32),
-            vmem((nr, 8, GROUPS), F32),
+            vmem((ny, 8, GROUPS), F32),
+            vmem((nz, 8, GROUPS), F32),
             vmem((2, 8, GROUPS), F32),
         ] + sems,
         compiler_params=pltpu.CompilerParams(

time: 67 us -> 68 us (1.015)
  Pallas kernels: 66.1 us -> 67.1 us
    pallas_call x1, Pallas kernels: 64.7 us -> 65.7 us  [local(): pl.pallas_call(functools.partial(kernel, nz, ny, nc, scale, wave_scale),...]
where the time goes in v6:
time: 68 us; the launch traced here: 67.7 us
  Pallas kernels  67.1 us (99%)
    pallas_call x1, Pallas kernels, local(): pl.pallas_call(functools.partial(kernel, nz, ny, nc, scale, wave_scale),...  65.7 us
    pallas_call x1, Pallas kernels, local(): pl.pallas_call(hand_out, out_shape=shapes, in_specs=[hbm] * 3, out_specs=...  1.37 us

profile of v6, /device:TPU:1, one launch (start us, length us, event | category | flops | bytes accessed | tf_op | source)
XLA Modules:
  0.0 67.7 jit_solution(14936241523558659669)
XLA Ops:
  0.6 65.7 %shard_map.121 = (f32[16,128]{1,0:T(8,128)}, bf16[16,32]{1,0:T(8,128)(2,1)}, f32[16,128]{1,0:T(8,128)}) custom-call(f32[3,128]{1,0:T(4,128)} %xyz_h.1, f32[1,128]{1,0:T(1,128)} %weight_h.1, f32[1,128]{1,0:T(1,128)} %bitcast.3, s32[1,128]{1,0:T(1,128)} %bitcast.4, f32[64,128]{1,0:T(8,128)} %binv_h.1, f32[16,128]{1,0:T(8,128)} %inc_h.1, f32[3,512]{1,0:T(4,128)} %fxyz_h.1, ...), custom_call_target="tpu_custom_call" | custom-call | tf_op jit(solution)/shard_map/pallas_call | solution.py:417
  66.4 1.4 %shard_map.122 = (f32[16,128]{1,0:T(8,128)}, bf16[16,32]{1,0:T(8,128)(2,1)}, f32[16,128]{1,0:T(8,128)}) custom-call(f32[16,128]{1,0:T(8,128)} %get-tuple-element.6.a0, bf16[16,32]{1,0:T(8,128)(2,1)} %get-tuple-element.7.a1, f32[16,128]{1,0:T(8,128)} %get-tuple-element.8.a2), custom_call_target="tpu_custom_call" | custom-call | tf_op jit(solution)/shard_map/pallas_call | solution.py:456

commit v7 on v5

--- a/solution.py
+++ b/solution.py
@@ -190,20 +190,18 @@
 
     acc[...] = jnp.zeros_like(acc)
 
-    each(1, nc, lambda k: arrived(k, tgt, tgt_rs))
-    for k in range(0, nc, 4):
-        feat_a[:, k * SH:(k + 4) * SH] = features_a(jnp.concatenate([tgt[n] for n in range(k, k + 4)], axis=1))
-
     def tile(b):
         return pair_values(jnp.dot(b, feat_a[...], preferred_element_type=F32))
 
     def source_features(c):
         return features_b(jnp.concatenate([src[2 * c, 0:16, :], src[2 * c + 1, 0:16, :]], axis=1))
 
-    def use(c):
+    def use(c, last=False):
         x = jnp.concatenate([src[2 * c, 16:32, :], src[2 * c + 1, 16:32, :]], axis=1)
         g = gbuf[...]
         acc[...] += jnp.dot(x, g, preferred_element_type=F32)
+        if last:
+            return
         back = lax.dot_general(xt[...], g, over_lanes, preferred_element_type=F32).astype(BF16)
         rsr_out[2 * c] = back[:, 0:SH]
         rsr_out[2 * c + 1] = back[:, SH:2 * SH]
@@ -230,14 +228,18 @@
                 row_copy(order[k], k, rsr_out.at[k], rsr_in.at[k], rsr_ss, rsr_rs).start()
 
     wait_chunk(0)
+    first = source_features(0)
     wait_chunk(1)
-    gbuf[...] = tile(source_features(0))
     feat_b[...] = source_features(1)
+    each(1, nc, lambda k: arrived(k, tgt, tgt_rs))
+    for k in range(0, nc, 4):
+        feat_a[:, k * SH:(k + 4) * SH] = features_a(jnp.concatenate([tgt[n] for n in range(k, k + 4)], axis=1))
+    gbuf[...] = tile(first)
     each(1, nc, lambda k: arrived(k, tgx, tgx_rs))
     for k in range(nc):
         xt[:, k * SH:(k + 1) * SH] = tgx[k]
     each(1, chunks, images_chunk)
-    use(chunks - 1)
+    use(chunks - 1, last=True)
 
     def rs_send(k):
         rs_out[k] = acc[:, pl.ds(pl.multiple_of(k * SH, SH), SH)].astype(BF16)

time: 67 us -> 66.8 us (level)
  no operation moved by 1% of the time
where the time goes in v7:
time: 66.8 us; the launch traced here: 66.5 us
  Pallas kernels  65.9 us (99%)
    pallas_call x1, Pallas kernels, local(): pl.pallas_call(functools.partial(kernel, nz, ny, nc, scale, wave_scale),...  64.5 us
    pallas_call x1, Pallas kernels, local(): pl.pallas_call(hand_out, out_shape=shapes, in_specs=[hbm] * 3, out_specs=...  1.37 us

profile of v7, /device:TPU:1, one launch (start us, length us, event | category | flops | bytes accessed | tf_op | source)
XLA Modules:
  0.0 66.5 jit_solution(6150689865906116425)
XLA Ops:
  0.6 64.5 %shard_map.121 = (f32[16,128]{1,0:T(8,128)}, bf16[16,32]{1,0:T(8,128)(2,1)}, f32[16,128]{1,0:T(8,128)}) custom-call(f32[3,128]{1,0:T(4,128)} %xyz_h.1, f32[1,128]{1,0:T(1,128)} %weight_h.1, f32[1,128]{1,0:T(1,128)} %bitcast.3, s32[1,128]{1,0:T(1,128)} %bitcast.4, f32[64,128]{1,0:T(8,128)} %binv_h.1, f32[16,128]{1,0:T(8,128)} %inc_h.1, f32[3,512]{1,0:T(4,128)} %fxyz_h.1, ...), custom_call_target="tpu_custom_call" | custom-call | tf_op jit(solution)/shard_map/pallas_call | solution.py:409
  65.2 1.4 %shard_map.122 = (f32[16,128]{1,0:T(8,128)}, bf16[16,32]{1,0:T(8,128)(2,1)}, f32[16,128]{1,0:T(8,128)}) custom-call(f32[16,128]{1,0:T(8,128)} %get-tuple-element.6.a0, bf16[16,32]{1,0:T(8,128)(2,1)} %get-tuple-element.7.a1, f32[16,128]{1,0:T(8,128)} %get-tuple-element.8.a2), custom_call_target="tpu_custom_call" | custom-call | tf_op jit(solution)/shard_map/pallas_call | solution.py:447
